TPU v7x, 32 devices: a whole 2x2x4 slice. The times are simulated.
32 devices in a mesh: gx: 8 (over z, x), gy: 4 (over y, core).
Axes of the slice: x: 2, y: 2, z: 4, core: 2. Of those that a mesh axis runs over, the one named last changes fastest.
Arguments:
- object_field: float32 [2, 2048, 1024], P(None, 'gx', 'gy'), may hold values from -4.5 to 4.5
- probe_field: float32 [2, 2, 256, 256], replicated, may hold values from -4.2 to 4.2
- amplitude: float32 [32, 4, 256, 256], P('gx', 'gy'), may hold values from 0.2 to 3
- offsets: int32 [32, 4, 2], P('gx', 'gy'), may hold values from -128 to 128
Outputs:
- updated_object: float32 [2, 2048, 1024], P(None, 'gx', 'gy')
- updated_probe: float32 [2, 2, 256, 256], replicated
All inputs are finite; a program needn't handle non-finite values.
Results may differ from a plain program's by a relative error of at most 0.0006.
The roundings to bfloat16 on the way count: a program that leaves them out, or rounds other values in their place, can miss the bound.
Values sent between devices are 32-bit elements; how exact they have to be, the bound alone decides.
A program may use at most 64 MiB of HBM per device.

v0:
```python
import functools
import math

import jax
import jax.numpy as jnp
import numpy as np
from jax import lax
from jax.experimental import pallas as pl
from jax.experimental.pallas import tpu as pltpu
from jax.sharding import PartitionSpec as P

MESH = pl.DeviceIdType.MESH
VMEM = pl.BlockSpec(memory_space=pltpu.VMEM)
ANY = pl.BlockSpec(memory_space=pl.ANY)
F32 = jnp.float32
BF16 = jnp.bfloat16
CHUNK = 32
SUB = 8
STRIPS = 4
PIECES = 8
MIDS = 4


def dft_tables(extent):
    indices = np.arange(extent)
    angles = (indices[:, None] * indices[None, :] % extent) * (2.0 * math.pi / extent)
    norm_factor = 1.0 / math.sqrt(extent)
    both = np.concatenate([np.cos(angles), np.sin(angles)], 1) * norm_factor
    return jnp.asarray(both.astype(np.float32).astype(jnp.bfloat16))


def remote(src, dst, sems, slot, device):
    return pltpu.make_async_remote_copy(
        src_ref=src,
        dst_ref=dst,
        send_sem=sems.at[0, slot],
        recv_sem=sems.at[1, slot],
        device_id=device,
        device_id_type=MESH,
    )


def greet(devices):
    barrier = pltpu.get_barrier_semaphore()
    for device in devices:
        pl.semaphore_signal(barrier, inc=1, device_id=device, device_id_type=MESH)
    pl.semaphore_wait(barrier, len(devices))


def halo_kernel(n_gx, n_gy, margin, obj, ext, sems, local_sem):
    gx, gy = lax.axis_index("gx"), lax.axis_index("gy")
    rows, cols = obj.shape[1], obj.shape[2]
    m = margin
    up = (lax.rem(gx + n_gx - 1, n_gx), gy)
    down = (lax.rem(gx + 1, n_gx), gy)
    left = (gx, lax.rem(gy + n_gy - 1, n_gy))
    right = (gx, lax.rem(gy + 1, n_gy))
    own = pltpu.make_async_copy(
        obj, ext.at[:, pl.ds(m, rows), pl.ds(m, cols)], local_sem.at[0]
    )
    own.start()
    greet((up, down, left, right))
    lcol, rcol = pl.ds(0, m), pl.ds(m + cols, m)
    mid_r, mid_c = pl.ds(m, rows), pl.ds(m, cols)
    piece = m // STRIPS
    slot = [0]

    def send(src, dst, device):
        copy = remote(src, dst, sems, slot[0], device)
        slot[0] += 1
        copy.start()
        return copy

    vertical = []
    for i in range(STRIPS):
        at = i * piece
        for src, dst, device in ((rows - m + at, at, down), (at, m + rows + at, up)):
            band = pl.ds(dst, piece)
            copy = send(obj.at[:, pl.ds(src, piece), :], ext.at[:, band, mid_c], device)
            vertical.append((copy, band))
    pending = [
        send(obj.at[:, :, pl.ds(cols - m, m)], ext.at[:, mid_r, lcol], right),
        send(obj.at[:, :, pl.ds(0, m)], ext.at[:, mid_r, rcol], left),
    ]
    for copy, band in vertical:
        copy.wait_recv()
        pending.append(send(ext.at[:, band, pl.ds(cols, m)], ext.at[:, band, lcol], right))
        pending.append(send(ext.at[:, band, pl.ds(m, m)], ext.at[:, band, rcol], left))
    for copy in pending:
        copy.wait_recv()
    for copy in pending:
        copy.wait_send()
    for copy, _ in vertical:
        copy.wait_send()
    own.wait()


def update_kernel(
    margin, offs, ext, probe, amp, table, acc, sums, win, psi, xbuf, ybuf, far, fr, frt
):
    p = pl.program_id(0)
    extent = probe.shape[-1]
    modes = probe.shape[0]
    width = ext.shape[2]
    r0 = offs[p, 0, 0] + margin
    c0 = offs[p, 0, 1] + margin
    back_shift = lax.rem(width - c0, width)
    low = lax.rem(r0, SUB)
    base = r0 - low
    tall = CHUNK + SUB
    row_shift = lax.rem(tall - low, tall)
    n_chunks = extent // CHUNK

    @pl.when(p == 0)
    def _():
        acc[...] = jnp.zeros_like(acc)
        sums[...] = jnp.zeros_like(sums)
        c, s = table[:, :extent], table[:, extent:]
        fr[:extent, :extent] = c
        fr[:extent, extent:] = s
        fr[extent:, :extent] = -s
        fr[extent:, extent:] = c
        frt[:extent, :extent] = c
        frt[:extent, extent:] = -s
        frt[extent:, :extent] = s
        frt[extent:, extent:] = c

    @pl.loop(0, n_chunks, unroll=8)
    def _(i):
        rb = pl.multiple_of(i * CHUNK, CHUNK)
        here = pl.ds(rb, CHUNK)
        w = []
        for part in range(2):
            line = ext[part, pl.ds(pl.multiple_of(base + rb, SUB), tall), :]
            line = pltpu.roll(line, row_shift, 0)[:CHUNK]
            w.append(pltpu.roll(line, back_shift, 1)[:, :extent])
            win[part, here, :] = w[part]
        sums[2 * modes, here, :] += w[0] * w[0] + w[1] * w[1]
        for k in range(modes):
            cols = slice(k * extent, (k + 1) * extent)
            pr, pi = probe[k, 0, here, :], probe[k, 1, here, :]
            psi_re = pr * w[0] - pi * w[1]
            psi_im = pr * w[1] + pi * w[0]
            psi[k, 0, here, :] = psi_re
            psi[k, 1, here, :] = psi_im
            xbuf[here, cols] = psi_re.astype(BF16)
            xbuf[pl.ds(extent + rb, CHUNK), cols] = psi_im.astype(BF16)

    def rows_then_cols(row_table, col_table):
        for part in range(2):
            table = row_table[part * extent : (part + 1) * extent, :]
            out = jnp.dot(table, xbuf[...], preferred_element_type=F32).astype(BF16)
            for k in range(modes):
                ybuf[k * extent : (k + 1) * extent, part * extent : (part + 1) * extent] = out[
                    :, k * extent : (k + 1) * extent
                ]
        for k in range(modes):
            band = slice(k * extent, (k + 1) * extent)
            far[band, :] = jnp.dot(ybuf[band, :], col_table[...], preferred_element_type=F32)

    rows_then_cols(fr, frt)

    @pl.loop(0, n_chunks, unroll=8)
    def _(i):
        rb = pl.multiple_of(i * CHUNK, CHUNK)
        parts = []
        intensity = jnp.zeros((CHUNK, extent), F32)
        for k in range(modes):
            at = pl.ds(k * extent + rb, CHUNK)
            re, im = far[at, :extent], far[at, extent:]
            intensity += re * re + im * im
            parts.append((re, im))
        factor = amp[0, pl.ds(rb, CHUNK), :] * jnp.minimum(lax.rsqrt(intensity), 4.0)
        for k in range(modes):
            cols = slice(k * extent, (k + 1) * extent)
            xbuf[pl.ds(rb, CHUNK), cols] = (parts[k][0] * factor).astype(BF16)
            xbuf[pl.ds(extent + rb, CHUNK), cols] = (parts[k][1] * factor).astype(BF16)

    rows_then_cols(frt, fr)

    @pl.loop(0, n_chunks, unroll=8)
    def _(i):
        rb = pl.multiple_of(i * CHUNK, CHUNK)
        here = pl.ds(rb, CHUNK)
        wr, wi = win[0, here, :], win[1, here, :]
        obj_re = jnp.zeros((CHUNK, extent), F32)
        obj_im = jnp.zeros((CHUNK, extent), F32)
        for k in range(modes):
            at = pl.ds(k * extent + rb, CHUNK)
            dr = far[at, :extent] - psi[k, 0, here, :]
            di = far[at, extent:] - psi[k, 1, here, :]
            pr, pi = probe[k, 0, here, :], probe[k, 1, here, :]
            obj_re += pr * dr + pi * di
            obj_im += pr * di - pi * dr
            sums[2 * k, here, :] += wr * dr + wi * di
            sums[2 * k + 1, here, :] += wr * di - wi * dr
        blank = jnp.zeros((CHUNK, width - extent), F32)
        below = jnp.zeros((SUB, width), F32)
        for part, value in enumerate((obj_re, obj_im)):
            line = pltpu.roll(jnp.concatenate([value, blank], 1), lax.rem(c0, width), 1)
            line = pltpu.roll(jnp.concatenate([line, below], 0), low, 0)
            acc[part, pl.ds(pl.multiple_of(base + rb, SUB), tall), :] += line


def reduce_plan(n_gx, n_gy):
    x_bits, y_bits = n_gx.bit_length() - 1, n_gy.bit_length() - 1
    core, x, y = ("gy", 0, 1), ("gx", 0, 1), ("gy", 1, 1)
    z = ("gx", 1, min(2, x_bits - 1))
    rest = [("gx", b, 1) for b in range(3, x_bits)] + [("gy", b, 1) for b in range(2, y_bits)]
    return ([core, x, y, z] + rest, [core, y, x, z] + rest)


def fold_kernel(n_gx, n_gy, margin, acc, obj, probe, sums, out_obj, out_probe, *scratch):
    (from_left, from_right, send_up, send_down, from_up, from_down, part, inbox, sems) = scratch
    gx, gy = lax.axis_index("gx"), lax.axis_index("gy")
    rows, cols = obj.shape[1], obj.shape[2]
    planes, extent = sums.shape[0], sums.shape[1]
    modes = probe.shape[0]
    m = margin
    up = (lax.rem(gx + n_gx - 1, n_gx), gy)
    down = (lax.rem(gx + 1, n_gx), gy)
    left = (gx, lax.rem(gy + n_gy - 1, n_gy))
    right = (gx, lax.rem(gy + 1, n_gy))
    plan = reduce_plan(n_gx, n_gy)

    def members(axis, bit, count):
        size, step = 1 << count, 1 << bit
        coord = gx if axis == "gx" else gy
        mine = lax.rem(coord // step, size)
        peers = []
        for d in range(1, size):
            field = lax.rem(mine + d, size)
            other = coord + step * (field - mine)
            peers.append((field, (other, gy) if axis == "gx" else (gx, other)))
        return size, mine, peers

    greet([up, down, left, right] + [dev for g in plan[0] for _, dev in members(*g)[2]])

    slot = [0]
    pending = []

    def send(src, dst, device):
        copy = remote(src, dst, sems, slot[0], device)
        slot[0] += 1
        copy.start()
        pending.append(copy)
        return copy

    lcol, rcol = pl.ds(0, m), pl.ds(m + cols, m)
    bands = (pl.ds(0, m), pl.ds(m + rows, m))
    mid = pl.ds(m, rows)

    def strip(band):
        return (
            send(acc.at[:, band, lcol], from_right.at[:, band, :], left),
            send(acc.at[:, band, rcol], from_left.at[:, band, :], right),
        )

    lanes = len(plan)
    lane_w = extent // lanes
    state = [{"off": 0, "n": extent, "src": sums, "box": 0} for _ in range(lanes)]
    history = [[] for _ in range(lanes)]

    def reduce_start(step):
        started = []
        for lane in range(lanes):
            s = state[lane]
            size, mine, peers = members(*plan[lane][step])
            at = pl.ds(lane * lane_w, lane_w)
            split = s["n"] % (size * SUB) == 0
            n = s["n"] // size if split else s["n"]
            copies = []
            for field, device in peers:
                give = s["off"] + field * n if split else s["off"]
                src = s["src"].at[:, pl.ds(pl.multiple_of(give, SUB), n), at]
                box = inbox.at[:, pl.ds(pl.multiple_of(s["box"] + mine * n, SUB), n), at]
                copies.append(send(src, box, device))
            keep = s["off"] + mine * n if split else s["off"]
            history[lane].append((size, mine, peers, split))
            started.append((copies, keep, n, size, mine, s["box"]))
            s["box"] += size * n
        return started

    def reduce_end(step, started):
        for lane, (copies, keep, n, size, mine, box) in enumerate(started):
            s = state[lane]
            at = pl.ds(lane * lane_w, lane_w)
            own = s["src"][:, pl.ds(pl.multiple_of(keep, SUB), n), at]
            inbox[:, pl.ds(pl.multiple_of(box + mine * n, SUB), n), at] = own
            for copy in copies:
                copy.wait_recv()
            total = inbox[:, pl.ds(box, n), at]
            for j in range(1, size):
                total += inbox[:, pl.ds(box + j * n, n), at]
            part[step, :, pl.ds(pl.multiple_of(keep, SUB), n), at] = total
            s["off"], s["n"], s["src"] = keep, n, part.at[step]

    def fold_band(copies, band, buf):
        for copy in copies:
            copy.wait_recv()
        buf[:, :, :m] = acc[:, band, pl.ds(m, m)] + from_left[:, band, :]
        if cols > 2 * m:
            buf[:, :, m : cols - m] = acc[:, band, pl.ds(2 * m, cols - 2 * m)]
        buf[:, :, cols - m :] = acc[:, band, pl.ds(cols, m)] + from_right[:, band, :]

    piece = m // PIECES
    folded = []

    def vertical(ups, downs):
        for i in ups:
            at = pl.ds(i * piece, piece)
            folded.append(send(send_up.at[:, at, :], from_down.at[:, at, :], up))
        for i in downs:
            at = pl.ds(i * piece, piece)
            folded.append(send(send_down.at[:, at, :], from_up.at[:, at, :], down))

    def middle(i):
        folded.extend(strip(pl.ds(m + i * (rows // MIDS), rows // MIDS)))

    started = reduce_start(0)
    corner_up = strip(bands[0])
    reduce_end(0, started)
    started = reduce_start(1)
    corner_down = strip(bands[1])
    fold_band(corner_up, bands[0], send_up)
    vertical((0, 1), ())
    reduce_end(1, started)
    started = reduce_start(2)
    fold_band(corner_down, bands[1], send_down)
    vertical((2, 3), (0, 1))
    middle(0)
    reduce_end(2, started)
    steps = len(plan[0])
    started = reduce_start(3)
    vertical((4, 5), (2, 3))
    middle(1)
    reduce_end(3, started)
    for step in range(4, steps):
        started = reduce_start(step)
        reduce_end(step, started)

    for lane in range(lanes):
        s = state[lane]
        at = pl.ds(lane * lane_w, lane_w)
        keep = pl.ds(pl.multiple_of(s["off"], SUB), s["n"])
        weight = s["src"][planes - 1, keep, at] + 1e-05
        for k in range(2 * modes):
            out_probe[k, keep, at] = s["src"][k, keep, at] / weight

    def gather_start(level):
        started = []
        for lane in range(lanes):
            s = state[lane]
            size, mine, peers, split = history[lane][level]
            at = pl.ds(lane * lane_w, lane_w)
            if split:
                own = out_probe.at[:, pl.ds(pl.multiple_of(s["off"], SUB), s["n"]), at]
                started += [send(own, own, device) for _, device in peers]
                s["off"] = s["off"] - mine * s["n"]
                s["n"] *= size
        return started

    def gather_end(started):
        for copy in started:
            copy.wait_recv()

    started = gather_start(steps - 1)
    vertical((6, 7), (4, 5))
    middle(2)
    power = jnp.zeros((extent, extent), F32)
    for k in range(modes):
        for c in range(2):
            power += probe[k, c] * probe[k, c]
    scale = jnp.max(power, keepdims=True) + 1e-06
    for level in range(steps - 2, 0, -1):
        gather_end(started)
        started = gather_start(level)
        if level == 2:
            vertical((), (6, 7))
            middle(3)
    gather_end(started)
    started = gather_start(0)
    for copy in folded:
        copy.wait_recv()
    for c in range(2):
        step_sum = acc[c, pl.ds(m, rows), pl.ds(m, cols)]
        gap_r = [jnp.zeros((rows - 2 * m, cols), F32)] if rows > 2 * m else []
        gap_c = [jnp.zeros((rows, cols - 2 * m), F32)] if cols > 2 * m else []
        side = jnp.concatenate(
            [from_left[c, pl.ds(m, rows), :]] + gap_c + [from_right[c, pl.ds(m, rows), :]], 1
        )
        ends = jnp.concatenate([from_up[c]] + gap_r + [from_down[c]], 0)
        out_obj[c] = (step_sum + side + ends) / scale
    gather_end(started)
    for copy in pending:
        copy.wait_send()


def body(n_gx, n_gy, object_field, probe_field, amplitude, offsets):
    extent = probe_field.shape[-1]
    modes = probe_field.shape[0]
    margin = extent // 2
    rows, cols = object_field.shape[1:]
    positions = amplitude.shape[0]
    ext_shape = (2, rows + 2 * margin + SUB, cols + 2 * margin)
    ext = pl.pallas_call(
        functools.partial(halo_kernel, n_gx, n_gy, margin),
        out_shape=jax.ShapeDtypeStruct(ext_shape, F32),
        in_specs=[ANY],
        out_specs=VMEM,
        scratch_shapes=[pltpu.SemaphoreType.DMA((2, 2 + 6 * STRIPS)), pltpu.SemaphoreType.DMA((1,))],
        compiler_params=pltpu.CompilerParams(collective_id=0, has_side_effects=True),
        name="halo",
    )(object_field)

    planes = 2 * modes + 1
    acc, sums = pl.pallas_call(
        functools.partial(update_kernel, margin),
        grid=(positions,),
        out_shape=(
            jax.ShapeDtypeStruct(ext_shape, F32),
            jax.ShapeDtypeStruct((planes, extent, extent), F32),
        ),
        in_specs=[
            pl.BlockSpec(memory_space=pltpu.SMEM),
            VMEM,
            VMEM,
            pl.BlockSpec((1, extent, extent), lambda i: (i, 0, 0)),
            VMEM,
        ],
        out_specs=(VMEM, VMEM),
        scratch_shapes=[
            pltpu.VMEM((2, extent, extent), F32),
            pltpu.VMEM((modes, 2, extent, extent), F32),
            pltpu.VMEM((2 * extent, modes * extent), BF16),
            pltpu.VMEM((modes * extent, 2 * extent), BF16),
            pltpu.VMEM((modes * extent, 2 * extent), F32),
            pltpu.VMEM((2 * extent, 2 * extent), BF16),
            pltpu.VMEM((2 * extent, 2 * extent), BF16),
        ],
        name="update",
    )(offsets, ext, probe_field, amplitude[:, 0], dft_tables(extent))

    plan = reduce_plan(n_gx, n_gy)[0]
    steps = len(plan)
    peers = sum((1 << count) - 1 for _, _, count in plan)
    out_obj, out_probe = pl.pallas_call(
        functools.partial(fold_kernel, n_gx, n_gy, margin),
        out_shape=(
            jax.ShapeDtypeStruct(object_field.shape, F32),
            jax.ShapeDtypeStruct((2 * modes, extent, extent), F32),
        ),
        in_specs=[VMEM] * 4,
        out_specs=(VMEM, VMEM),
        scratch_shapes=[
            pltpu.VMEM((2, rows + 2 * margin, margin), F32),
            pltpu.VMEM((2, rows + 2 * margin, margin), F32),
            pltpu.VMEM((2, margin, cols), F32),
            pltpu.VMEM((2, margin, cols), F32),
            pltpu.VMEM((2, margin, cols), F32),
            pltpu.VMEM((2, margin, cols), F32),
            pltpu.VMEM((steps, planes, extent, extent), F32),
            pltpu.VMEM((planes, 3 * extent, extent), F32),
            pltpu.SemaphoreType.DMA((2, 4 + 2 * PIECES + 2 * MIDS + 4 * peers)),
        ],
        compiler_params=pltpu.CompilerParams(collective_id=1, has_side_effects=True),
        name="fold",
    )(acc, object_field, probe_field, sums)
    return object_field + out_obj, probe_field + out_probe.reshape(probe_field.shape)


def solution(mesh):
    in_specs = (P(None, "gx", "gy"), P(), P("gx", "gy", None, None), P("gx", "gy", None))
    out_specs = (P(None, "gx", "gy"), P())
    step = functools.partial(body, mesh.shape["gx"], mesh.shape["gy"])
    return jax.shard_map(step, mesh=mesh, in_specs=in_specs, out_specs=out_specs, check_vma=False)
```

profile of v0, /device:TPU:0, one launch (start us, length us, event | category | flops | bytes accessed | tf_op | source)
XLA Modules:
  0.0 83.0 jit_solution(654055234844414626)
XLA Ops:
  0.6 1.3 %copy.7.offs = s32[4,1,2]{2,1,0:T(1,128)} copy(s32[4,1,2]{0,2,1:T(2,128)} %param.8) | data formatting | bytes 64 | tf_op args[3]
  2.0 20.3 %halo.1.ext = f32[2,520,512]{2,1,0:T(8,128)} custom-call(f32[2,256,256]{2,1,0:T(8,128)} %obj.3), custom_call_target="tpu_custom_call" | custom-call | tf_op jit(solution)/shard_map/halo/pallas_call | solution.py:406
  22.3 13.6 %update.1 = (f32[2,520,512]{2,1,0:T(8,128)}, f32[5,256,256]{2,1,0:T(8,128)}) custom-call(s32[4,1,2]{2,1,0:T(1,128)} %copy.7.offs, f32[2,520,512]{2,1,0:T(8,128)} %halo.1.ext, f32[2,2,256,256]{3,2,1,0:T(8,128)} %probe.3, f32[4,256,256]{2,1,0:T(8,128)} %bitcast.3, bf16[256,512]{1,0:T(8,128)(2,1)} %constant.2.clone.table), custom_call_target="tpu_custom_call" | custom-call | tf_op jit(solution)/shard_map/update/pallas_call | solution.py:417
  35.9 0.0 copy-start.1
  35.9 0.0 copy-start
  35.9 44.0 %fold.1 = (f32[2,256,256]{2,1,0:T(8,128)}, f32[4,256,256]{2,1,0:T(8,128)}) custom-call(f32[2,520,512]{2,1,0:T(8,128)} %get-tuple-element.6.acc, f32[2,256,256]{2,1,0:T(8,128)} %obj.3, f32[2,2,256,256]{3,2,1,0:T(8,128)} %probe.3, f32[5,256,256]{2,1,0:T(8,128)} %get-tuple-element.7.sums), custom_call_target="tpu_custom_call" | custom-call | tf_op jit(solution)/shard_map/fold/pallas_call | solution.py:447
  79.9 0.0 copy-start.2
  79.9 0.0 copy-done.1
  79.9 2.0 %add.6 = f32[2,256,256]{2,1,0:T(8,128)} add(f32[2,256,256]{2,1,0:T(8,128)S(1)} %copy-done.1, f32[2,256,256]{2,1,0:T(8,128)} %get-tuple-element.8) | non-fusion elementwise | flops 131072 | bytes 1572864 | tf_op jit(solution)/shard_map/add | solution.py:469
  81.9 0.0 copy-done
  81.9 0.0 copy-done.2
  81.9 1.1 %add.7 = f32[2,2,256,256]{3,2,1,0:T(8,128)} add(f32[2,2,256,256]{3,2,1,0:T(8,128)S(1)} %copy-done, f32[2,2,256,256]{3,2,1,0:T(8,128)S(1)} %bitcast.2) | non-fusion elementwise | flops 262144 | bytes 3145728 | tf_op jit(solution)/shard_map/add | solution.py:469
Async XLA Ops:
  35.9 44.1 %copy-start.1 = (f32[2,256,256]{2,1,0:T(8,128)S(1)}, f32[2,256,256]{2,1,0:T(8,128)}, u32[]{:S(2)}) copy-start(f32[2,256,256]{2,1,0:T(8,128)} %obj.3) | copy-start | bytes 1572868
  35.9 46.1 %copy-start = (f32[2,2,256,256]{3,2,1,0:T(8,128)S(1)}, f32[2,2,256,256]{3,2,1,0:T(8,128)}, u32[]{:S(2)}) copy-start(f32[2,2,256,256]{3,2,1,0:T(8,128)} %probe.3) | copy-start | bytes 3145732
  79.9 2.0 %copy-start.2 = (f32[4,256,256]{2,1,0:T(8,128)S(1)}, f32[4,256,256]{2,1,0:T(8,128)}, u32[]{:S(2)}) copy-start(f32[4,256,256]{2,1,0:T(8,128)} %get-tuple-element.9) | copy-start | bytes 3145732
where the time goes:
time: 83.2 us; the launch traced here: 83 us
  Pallas kernels  77.9 us (94%)
  other arithmetic  3.09 us (4%)
  local copies, waits for them, and re-layouts  1.35 us (2%)
    pallas_call x1, Pallas kernels, body(): pl.pallas_call(functools.partial(fold_kernel, n_gx, n_gy, margin), out_sh...  44 us
    pallas_call x1, Pallas kernels, body(): pl.pallas_call(functools.partial(halo_kernel, n_gx, n_gy, margin), out_sh...  20.3 us
    pallas_call x1, Pallas kernels, body(): pl.pallas_call(functools.partial(update_kernel, margin), grid=(positions,...  13.6 us
    add x1, other arithmetic, body(): object_field + out_obj  1.99 us

commit v1 on v0

--- a/solution.py
+++ b/solution.py
@@ -19,6 +19,7 @@
 STRIPS = 4
 PIECES = 8
 MIDS = 4
+LIMIT = 30 << 20
 
 
 def dft_tables(extent):
@@ -102,8 +103,8 @@
     extent = probe.shape[-1]
     modes = probe.shape[0]
     width = ext.shape[2]
-    r0 = offs[p, 0, 0] + margin
-    c0 = offs[p, 0, 1] + margin
+    r0 = offs[0, 0, p] + margin
+    c0 = offs[0, 1, p] + margin
     back_shift = lax.rem(width - c0, width)
     low = lax.rem(r0, SUB)
     base = r0 - low
@@ -409,7 +410,7 @@
         in_specs=[ANY],
         out_specs=VMEM,
         scratch_shapes=[pltpu.SemaphoreType.DMA((2, 2 + 6 * STRIPS)), pltpu.SemaphoreType.DMA((1,))],
-        compiler_params=pltpu.CompilerParams(collective_id=0, has_side_effects=True),
+        compiler_params=pltpu.CompilerParams(collective_id=0, has_side_effects=True, vmem_limit_bytes=LIMIT),
         name="halo",
     )(object_field)
 
@@ -438,8 +439,9 @@
             pltpu.VMEM((2 * extent, 2 * extent), BF16),
             pltpu.VMEM((2 * extent, 2 * extent), BF16),
         ],
+        compiler_params=pltpu.CompilerParams(vmem_limit_bytes=LIMIT),
         name="update",
-    )(offsets, ext, probe_field, amplitude[:, 0], dft_tables(extent))
+    )(offsets.transpose(1, 2, 0), ext, probe_field, amplitude[:, 0], dft_tables(extent))
 
     plan = reduce_plan(n_gx, n_gy)[0]
     steps = len(plan)
@@ -463,7 +465,7 @@
             pltpu.VMEM((planes, 3 * extent, extent), F32),
             pltpu.SemaphoreType.DMA((2, 4 + 2 * PIECES + 2 * MIDS + 4 * peers)),
         ],
-        compiler_params=pltpu.CompilerParams(collective_id=1, has_side_effects=True),
+        compiler_params=pltpu.CompilerParams(collective_id=1, has_side_effects=True, vmem_limit_bytes=LIMIT),
         name="fold",
     )(acc, object_field, probe_field, sums)
     return object_field + out_obj, probe_field + out_probe.reshape(probe_field.shape)

time: 83.2 us -> 74.7 us (0.90)
  Pallas kernels: 77.9 us -> 70.7 us
  other arithmetic: 3.09 us -> 1.97 us
    pallas_call x1, Pallas kernels: 44 us -> 40.9 us  [body(): pl.pallas_call(functools.partial(fold_kernel, n_gx, n_gy, margin), out_sh...]
    pallas_call x1, Pallas kernels: 13.6 us -> 11 us  [body(): pl.pallas_call(functools.partial(update_kernel, margin), grid=(positions,...]
    pallas_call x1, Pallas kernels: 20.3 us -> 18.9 us  [body(): pl.pallas_call(functools.partial(halo_kernel, n_gx, n_gy, margin), out_sh...]
    add x1, other arithmetic: 1.99 us -> 0.86 us  [body(): object_field + out_obj]
where the time goes in v1:
time: 74.7 us; the launch traced here: 74.5 us
  Pallas kernels  70.7 us (95%)
  other arithmetic  1.97 us (3%)
  local copies, waits for them, and re-layouts  1.14 us (2%)
    pallas_call x1, Pallas kernels, body(): pl.pallas_call(functools.partial(fold_kernel, n_gx, n_gy, margin), out_sh...  40.9 us
    pallas_call x1, Pallas kernels, body(): pl.pallas_call(functools.partial(halo_kernel, n_gx, n_gy, margin), out_sh...  18.9 us
    pallas_call x1, Pallas kernels, body(): pl.pallas_call(functools.partial(update_kernel, margin), grid=(positions,...  11 us

profile of v1, /device:TPU:0, one launch (start us, length us, event | category | flops | bytes accessed | tf_op | source)
XLA Modules:
  0.0 74.5 jit_solution(16431937985555633145)
XLA Ops:
  0.6 0.0 copy-start
  0.6 0.0 copy-start.1
  0.7 1.1 %copy-done.1 = f32[2,256,256]{2,1,0:T(8,128)S(1)} copy-done((f32[2,256,256]{2,1,0:T(8,128)S(1)}, f32[2,256,256]{2,1,0:T(8,128)}, u32[]{:S(2)}) %copy-start.1) | copy-done | bytes 524312
  1.8 0.0 copy-start.2
  1.8 0.0 copy-start.3
  1.8 0.0 copy-start.4
  1.8 18.9 %halo.1.ext = f32[2,520,512]{2,1,0:T(8,128)S(1)} custom-call(f32[2,256,256]{2,1,0:T(8,128)S(1)} %copy-done.1), custom_call_target="tpu_custom_call" | custom-call | tf_op jit(solution)/shard_map/halo/pallas_call | solution.py:407
  20.6 0.0 copy-done
  20.6 0.0 copy-done.2
  20.7 0.0 copy-done.3
  20.7 0.0 copy-done.4
  20.7 11.0 %update.1 = (f32[2,520,512]{2,1,0:T(8,128)S(1)}, f32[5,256,256]{2,1,0:T(8,128)S(1)}) custom-call(s32[1,2,4]{2,1,0:T(2,128)S(1)} %bitcast.5, f32[2,520,512]{2,1,0:T(8,128)S(1)} %halo.1.ext, f32[2,2,256,256]{3,2,1,0:T(8,128)S(1)} %copy-done, f32[4,256,256]{2,1,0:T(8,128)S(1)} %bitcast.3, bf16[256,512]{1,0:T(8,128)(2,1)S(1)} %copy-done.3), custom_call_target="tpu_custom_call" | custom-call | tf_op jit(solution)/shard_map/update/pallas_call | solution.py:418
  31.7 40.9 %fold.1 = (f32[2,256,256]{2,1,0:T(8,128)S(1)}, f32[4,256,256]{2,1,0:T(8,128)S(1)}) custom-call(f32[2,520,512]{2,1,0:T(8,128)S(1)} %get-tuple-element.6.acc, f32[2,256,256]{2,1,0:T(8,128)S(1)} %copy-done.1, f32[2,2,256,256]{3,2,1,0:T(8,128)S(1)} %copy-done, f32[5,256,256]{2,1,0:T(8,128)S(1)} %get-tuple-element.7.sums), custom_call_target="tpu_custom_call" | custom-call | tf_op jit(solution)/shard_map/fold/pallas_call | solution.py:449
  72.5 0.9 %add.6 = f32[2,256,256]{2,1,0:T(8,128)} add(f32[2,256,256]{2,1,0:T(8,128)S(1)} %copy-done.1, f32[2,256,256]{2,1,0:T(8,128)S(1)} %get-tuple-element.8) | non-fusion elementwise | flops 131072 | bytes 1572864 | tf_op jit(solution)/shard_map/add | solution.py:471
  73.4 1.1 %add.7 = f32[2,2,256,256]{3,2,1,0:T(8,128)} add(f32[2,2,256,256]{3,2,1,0:T(8,128)S(1)} %copy-done, f32[2,2,256,256]{3,2,1,0:T(8,128)S(1)} %bitcast.4) | non-fusion elementwise | flops 262144 | bytes 3145728 | tf_op jit(solution)/shard_map/add | solution.py:471
Async XLA Ops:
  0.6 20.0 %copy-start = (f32[2,2,256,256]{3,2,1,0:T(8,128)S(1)}, f32[2,2,256,256]{3,2,1,0:T(8,128)}, u32[]{:S(2)}) copy-start(f32[2,2,256,256]{3,2,1,0:T(8,128)} %probe.3) | copy-start | bytes 3145732
  0.6 1.1 %copy-start.1 = (f32[2,256,256]{2,1,0:T(8,128)S(1)}, f32[2,256,256]{2,1,0:T(8,128)}, u32[]{:S(2)}) copy-start(f32[2,256,256]{2,1,0:T(8,128)} %obj.3) | copy-start | bytes 1572868
  1.8 18.9 %copy-start.2 = (f32[4,1,256,256]{3,2,1,0:T(8,128)S(1)}, f32[4,1,256,256]{3,2,1,0:T(8,128)}, u32[]{:S(2)}) copy-start(f32[4,1,256,256]{3,2,1,0:T(8,128)} %param.7) | copy-start | bytes 3145732
  1.8 18.9 %copy-start.3 = (bf16[256,512]{1,0:T(8,128)(2,1)S(1)}, bf16[256,512]{1,0:T(8,128)(2,1)}, u32[]{:S(2)}) copy-start(bf16[256,512]{1,0:T(8,128)(2,1)} %constant.2.clone.table) | copy-start | bytes 786436
  1.8 18.9 %copy-start.4 = (s32[4,1,2]{0,2,1:T(2,128)S(1)}, s32[4,1,2]{0,2,1:T(2,128)}, u32[]{:S(2)}) copy-start(s32[4,1,2]{0,2,1:T(2,128)} %param.8) | copy-start | bytes 100

commit v2 on v1

v2 whole, which is shorter than its diff:
```python
import functools
import math

import jax
import jax.numpy as jnp
import numpy as np
from jax import lax
from jax.experimental import pallas as pl
from jax.experimental.pallas import tpu as pltpu
from jax.sharding import PartitionSpec as P

MESH = pl.DeviceIdType.MESH
VMEM = pl.BlockSpec(memory_space=pltpu.VMEM)
HBM = pl.BlockSpec(memory_space=pltpu.MemorySpace.HBM)
F32 = jnp.float32
BF16 = jnp.bfloat16
CHUNK = 32
SUB = 8
STRIPS = 2
PIECES = 2
MIDS = 2
LIMIT = 30 << 20


def dft_tables(extent):
    indices = np.arange(extent)
    angles = (indices[:, None] * indices[None, :] % extent) * (2.0 * math.pi / extent)
    norm_factor = 1.0 / math.sqrt(extent)
    both = np.concatenate([np.cos(angles), np.sin(angles)], 1) * norm_factor
    return jnp.asarray(both.astype(np.float32).astype(jnp.bfloat16))


def remote(src, dst, sems, slot, device):
    return pltpu.make_async_remote_copy(
        src_ref=src,
        dst_ref=dst,
        send_sem=sems.at[0, slot],
        recv_sem=sems.at[1, slot],
        device_id=device,
        device_id_type=MESH,
    )


def greet(devices):
    barrier = pltpu.get_barrier_semaphore()
    for device in devices:
        pl.semaphore_signal(barrier, inc=1, device_id=device, device_id_type=MESH)
    pl.semaphore_wait(barrier, len(devices))


def halo_kernel(n_gx, n_gy, margin, obj, ext, sems, local_sem):
    gx, gy = lax.axis_index("gx"), lax.axis_index("gy")
    rows, cols = obj.shape[1], obj.shape[2]
    m = margin
    odd = lax.rem(gy, 2)
    up = (lax.rem(gx + n_gx - 1, n_gx), gy)
    down = (lax.rem(gx + 1, n_gx), gy)
    step_y = 1 - 2 * odd
    near = (gx, gy + step_y)
    far = (gx, lax.rem(gy - step_y + n_gy, n_gy))
    sides = (near, far)
    half_at = (pl.multiple_of((1 - odd) * (cols - m), m), pl.multiple_of(odd * (cols - m), m))
    lands_at = (pl.multiple_of(odd * (m + cols), m), pl.multiple_of((1 - odd) * (m + cols), m))
    own = pltpu.make_async_copy(obj, ext.at[:, pl.ds(m, rows), pl.ds(m, cols)], local_sem.at[0])
    own.start()
    greet((up, down, near, far))
    slot = [0]
    pending = []

    def send(src, dst, device):
        copy = remote(src, dst, sems, slot[0], device)
        slot[0] += 1
        copy.start()
        pending.append(copy)
        return copy

    piece = m // STRIPS
    ways = ((0, m + rows, up), (rows - m, 0, down))
    arrivals = []
    waits = []

    def middle(side):
        src = obj.at[:, :, pl.ds(half_at[side], m)]
        dst = ext.at[:, pl.ds(m, rows), pl.ds(lands_at[side], m)]
        waits.append(send(src, dst, sides[side]))

    def vertical(side):
        for i in range(STRIPS):
            for src_row, dst_row, device in ways:
                band = pl.ds(dst_row + i * piece, piece)
                src = obj.at[:, pl.ds(src_row + i * piece, piece), pl.ds(half_at[side], m)]
                dst = ext.at[:, band, pl.ds(m + half_at[side], m)]
                arrivals.append((send(src, dst, device), side, band))

    vertical(1)
    middle(1)
    vertical(0)
    middle(0)
    for copy, side, band in arrivals:
        copy.wait_recv()
        src = ext.at[:, band, pl.ds(m + half_at[side], m)]
        waits.append(send(src, ext.at[:, band, pl.ds(lands_at[side], m)], sides[side]))
    for copy in waits:
        copy.wait_recv()
    for copy in pending:
        copy.wait_send()
    own.wait()


def update_kernel(
    margin, offs, ext, probe, amp, table, acc, sums, win, psi, xbuf, ybuf, far, fr, frt
):
    p = pl.program_id(0)
    extent = probe.shape[-1]
    modes = probe.shape[0]
    width = ext.shape[2]
    r0 = offs[0, 0, p] + margin
    c0 = offs[0, 1, p] + margin
    back_shift = lax.rem(width - c0, width)
    low = lax.rem(r0, SUB)
    base = r0 - low
    tall = CHUNK + SUB
    row_shift = lax.rem(tall - low, tall)
    n_chunks = extent // CHUNK

    @pl.when(p == 0)
    def _():
        acc[...] = jnp.zeros_like(acc)
        sums[...] = jnp.zeros_like(sums)
        c, s = table[:, :extent], table[:, extent:]
        fr[:extent, :extent] = c
        fr[:extent, extent:] = s
        fr[extent:, :extent] = -s
        fr[extent:, extent:] = c
        frt[:extent, :extent] = c
        frt[:extent, extent:] = -s
        frt[extent:, :extent] = s
        frt[extent:, extent:] = c

    @pl.loop(0, n_chunks, unroll=8)
    def _(i):
        rb = pl.multiple_of(i * CHUNK, CHUNK)
        here = pl.ds(rb, CHUNK)
        w = []
        for part in range(2):
            line = ext[part, pl.ds(pl.multiple_of(base + rb, SUB), tall), :]
            line = pltpu.roll(line, row_shift, 0)[:CHUNK]
            w.append(pltpu.roll(line, back_shift, 1)[:, :extent])
            win[part, here, :] = w[part]
        sums[0, here, :] += w[0] * w[0] + w[1] * w[1]
        for k in range(modes):
            cols = slice(k * extent, (k + 1) * extent)
            pr, pi = probe[k, 0, here, :], probe[k, 1, here, :]
            psi_re = pr * w[0] - pi * w[1]
            psi_im = pr * w[1] + pi * w[0]
            psi[k, 0, here, :] = psi_re
            psi[k, 1, here, :] = psi_im
            xbuf[here, cols] = psi_re.astype(BF16)
            xbuf[pl.ds(extent + rb, CHUNK), cols] = psi_im.astype(BF16)

    def rows_then_cols(row_table, col_table):
        for part in range(2):
            table = row_table[part * extent : (part + 1) * extent, :]
            out = jnp.dot(table, xbuf[...], preferred_element_type=F32).astype(BF16)
            for k in range(modes):
                ybuf[k * extent : (k + 1) * extent, part * extent : (part + 1) * extent] = out[
                    :, k * extent : (k + 1) * extent
                ]
        for k in range(modes):
            band = slice(k * extent, (k + 1) * extent)
            far[band, :] = jnp.dot(ybuf[band, :], col_table[...], preferred_element_type=F32)

    rows_then_cols(fr, frt)

    @pl.loop(0, n_chunks, unroll=8)
    def _(i):
        rb = pl.multiple_of(i * CHUNK, CHUNK)
        parts = []
        intensity = jnp.zeros((CHUNK, extent), F32)
        for k in range(modes):
            at = pl.ds(k * extent + rb, CHUNK)
            re, im = far[at, :extent], far[at, extent:]
            intensity += re * re + im * im
            parts.append((re, im))
        factor = amp[0, pl.ds(rb, CHUNK), :] * jnp.minimum(lax.rsqrt(intensity), 4.0)
        for k in range(modes):
            cols = slice(k * extent, (k + 1) * extent)
            xbuf[pl.ds(rb, CHUNK), cols] = (parts[k][0] * factor).astype(BF16)
            xbuf[pl.ds(extent + rb, CHUNK), cols] = (parts[k][1] * factor).astype(BF16)

    rows_then_cols(frt, fr)

    @pl.loop(0, n_chunks, unroll=8)
    def _(i):
        rb = pl.multiple_of(i * CHUNK, CHUNK)
        here = pl.ds(rb, CHUNK)
        wr, wi = win[0, here, :], win[1, here, :]
        obj_re = jnp.zeros((CHUNK, extent), F32)
        obj_im = jnp.zeros((CHUNK, extent), F32)
        for k in range(modes):
            at = pl.ds(k * extent + rb, CHUNK)
            dr = far[at, :extent] - psi[k, 0, here, :]
            di = far[at, extent:] - psi[k, 1, here, :]
            pr, pi = probe[k, 0, here, :], probe[k, 1, here, :]
            obj_re += pr * dr + pi * di
            obj_im += pr * di - pi * dr
            sums[2 * k + 1, here, :] += wr * dr + wi * di
            sums[2 * k + 2, here, :] += wr * di - wi * dr
        blank = jnp.zeros((CHUNK, width - extent), F32)
        below = jnp.zeros((SUB, width), F32)
        for part, value in enumerate((obj_re, obj_im)):
            line = pltpu.roll(jnp.concatenate([value, blank], 1), lax.rem(c0, width), 1)
            line = pltpu.roll(jnp.concatenate([line, below], 0), low, 0)
            acc[part, pl.ds(pl.multiple_of(base + rb, SUB), tall), :] += line


def reduce_plan(n_gx, n_gy):
    x_bits, y_bits = n_gx.bit_length() - 1, n_gy.bit_length() - 1
    steps = [(0, 0, 0, 1), (0, 1, 1, 1)]
    steps.append((1, min(2, x_bits - 1), 0, 0))
    for b in range(3, x_bits, 2):
        steps.append((b, min(2, x_bits - b), 0, 0))
    for b in range(2, y_bits, 2):
        steps.append((0, 0, b, min(2, y_bits - b)))
    return steps


def fold_schedule(steps, n):
    bands = [(b, i) for i in range(PIECES) for b in (0, 1)]
    near_bands = [("vert", 0, b, i) for b, i in bands]
    far_bands = [("vert", 1, b, i) for b, i in bands]
    half = len(far_bands) // 2
    acts = [("rs", 0, c) for c in range(n)]
    acts += [("corner", 0, b, i) for b, i in bands] + [("power",)]
    for c in range(n):
        acts += [("rse", 0, c), ("rs", 1, c)]
    acts += [("corner", 1, b, i) for b, i in bands] + near_bands
    for c in range(n):
        acts += [("rse", 1, c), ("rs", 2, c)]
    acts += [("mid", side, i, MIDS) for side in (1, 0) for i in range(MIDS)] + far_bands[:half]
    for s in range(2, steps):
        for c in range(n):
            acts.append(("rse", s, c))
            acts += [("rs", s + 1, c)] if s + 1 < steps else [("div", c), ("agz", c)]
    acts += far_bands[half:]
    for name in ("agp", "agc", "age"):
        acts += [(name, c) for c in range(n)]
    return acts + [("finish",)]


def fold_kernel(n_gx, n_gy, margin, chunks, acc, probe, sums, out_obj, out_probe, *scratch):
    (from_near, from_far, vsend, vrecv, part, inbox, sems) = scratch
    gx, gy = lax.axis_index("gx"), lax.axis_index("gy")
    rows, cols = out_obj.shape[1], out_obj.shape[2]
    planes, extent = sums.shape[0], sums.shape[1]
    modes = probe.shape[0]
    m = margin
    odd = lax.rem(gy, 2)
    up = (lax.rem(gx + n_gx - 1, n_gx), gy)
    down = (lax.rem(gx + 1, n_gx), gy)
    step_y = 1 - 2 * odd
    near = (gx, gy + step_y)
    far = (gx, lax.rem(gy - step_y + n_gy, n_gy))
    sides = (near, far)
    came = (from_near, from_far)
    halo_at = (pl.multiple_of((1 - odd) * (m + cols), m), pl.multiple_of(odd * (m + cols), m))
    half_at = (pl.multiple_of(m + (1 - odd) * (cols - m), m), pl.multiple_of(m + odd * (cols - m), m))
    plan = reduce_plan(n_gx, n_gy)
    steps = len(plan)

    def swap(field, d, bits):
        out = 0
        for b in range(bits):
            bit = lax.rem(field // (1 << b), 2)
            out = out + (1 << b) * (1 - bit if d >> b & 1 else bit)
        return out

    def members(bx, cx, by, cy):
        nx, ny = 1 << cx, 1 << cy
        fx, fy = lax.rem(gx // (1 << bx), nx), lax.rem(gy // (1 << by), ny)
        peers = []
        for dy in range(ny):
            for dx in range(nx):
                if dx or dy:
                    px, py = swap(fx, dx, cx), swap(fy, dy, cy)
                    peers.append((px + nx * py, (gx + (px - fx) * (1 << bx), gy + (py - fy) * (1 << by))))
        return nx * ny, fx + nx * fy, peers

    greet([up, down, near, far] + [dev for g in plan for _, dev in members(*g)[2]])

    slot = [0]
    pending = []

    def send(src, dst, device):
        copy = remote(src, dst, sems, slot[0], device)
        slot[0] += 1
        copy.start()
        pending.append(copy)
        return copy

    state = [{"off": 0, "n": extent, "src": sums, "box": 0} for _ in chunks]
    history = [[] for _ in chunks]
    flight = {}

    def rws(at, n):
        return pl.ds(pl.multiple_of(at, SUB), n)

    def rs(step, c):
        lo, hi = chunks[c]
        s = state[c]
        size, mine, peers = members(*plan[step])
        split = step < 3
        n = s["n"] // size if split else s["n"]
        copies = []
        for field, device in peers:
            give = s["off"] + field * n if split else s["off"]
            box = s["box"] + mine * n
            copies.append(send(s["src"].at[lo:hi, rws(give, n), :], inbox.at[lo:hi, rws(box, n), :], device))
        keep = s["off"] + mine * n if split else s["off"]
        history[c].append((size, mine, peers, split))
        flight["rs", step, c] = (copies, keep, n, size, mine, [f for f, _ in peers], s["box"], split)
        s["box"] += size * n

    def rse(step, c):
        lo, hi = chunks[c]
        copies, keep, n, size, mine, fields, box, split = flight.pop(("rs", step, c))
        s = state[c]
        for copy in copies:
            copy.wait_recv()
        own = s["src"][lo:hi, rws(keep, n), :]
        if split:
            total = own
            for f in fields:
                total += inbox[lo:hi, rws(box + f * n, n), :]
        else:
            inbox[lo:hi, rws(box + mine * n, n), :] = own
            total = inbox[lo:hi, rws(box, n), :]
            for j in range(1, size):
                total += inbox[lo:hi, rws(box + j * n, n), :]
        part[step, lo:hi, rws(keep, n), :] = total
        s["off"], s["n"], s["src"] = keep, n, part.at[step]

    def div(c):
        lo, hi = chunks[c]
        first = 1 if lo == 0 else 0
        s = state[c]
        keep = rws(s["off"], s["n"])
        weight = s["src"][0, keep, :] + 1e-05
        for k in range(lo + first, hi):
            out_probe[k - 1, keep, :] = s["src"][k, keep, :] / weight

    def planes_of(c):
        lo, hi = chunks[c][:2]
        return max(lo - 1, 0), hi - 1

    def give(c, off, n, device):
        lo, hi = planes_of(c)
        own = out_probe.at[lo:hi, rws(off, n), :]
        return send(own, own, device)

    def agz(c):
        off, n = state[c]["off"], state[c]["n"]
        _, _, z_peers, _ = history[c][2]
        _, _, p_peers, _ = history[c][1]
        zs = [give(c, off, n, device) for _, device in z_peers]
        ps = [[give(c, off, n, device)] for _, device in p_peers]
        flight["agz", c] = (zs, ps)

    def agp(c):
        off, n = state[c]["off"], state[c]["n"]
        z_size, z_mine, z_peers, _ = history[c][2]
        _, _, p_peers, _ = history[c][1]
        _, _, ((_, partner),), _ = history[c][0]
        zs, ps = flight.pop(("agz", c))
        base = off - z_mine * n
        for (field, _), copy in zip(z_peers, zs):
            copy.wait_recv()
            for (_, device), got in zip(p_peers, ps):
                got.append(give(c, base + field * n, n, device))
        flight["agp", c] = (ps, base, n * z_size, [give(c, base, n * z_size, partner)])

    def agc(c):
        ps, base, n, cs = flight.pop(("agp", c))
        p_size, p_mine, p_peers, _ = history[c][1]
        _, _, ((_, partner),), _ = history[c][0]
        for (field, _), copies in zip(p_peers, ps):
            for copy in copies:
                copy.wait_recv()
            cs.append(give(c, base + (field - p_mine) * n, n, partner))
        flight["agc", c] = cs

    def age(c):
        for copy in flight.pop(("agc", c)):
            copy.wait_recv()

    band_at = (0, m + rows)
    piece = m // PIECES

    def corner(side, b, i):
        band = pl.ds(band_at[b] + i * piece, piece)
        flight["corner", side, b, i] = send(acc.at[:, band, pl.ds(halo_at[side], m)], came[side].at[:, band, :], sides[side])

    def mid(side, i, of):
        band = pl.ds(m + i * (rows // of), rows // of)
        flight["mid", side, i] = send(acc.at[:, band, pl.ds(halo_at[side], m)], came[side].at[:, band, :], sides[side])

    def vert(side, b, i):
        flight.pop(("corner", side, b, i)).wait_recv()
        band = pl.ds(band_at[b] + i * piece, piece)
        here = pl.ds(i * piece, piece)
        vsend[b, side, :, here, :] = acc[:, band, pl.ds(half_at[side], m)] + came[side][:, band, :]
        flight["vert", side, b, i] = send(vsend.at[b, side, :, here, :], vrecv.at[b, side, :, here, :], (up, down)[b])

    power_box = []
    def power():
        total = jnp.zeros((extent, extent), F32)
        for k in range(modes):
            for c in range(2):
                total += probe[k, c] * probe[k, c]
        power_box.append(jnp.max(total, keepdims=True) + 1e-06)

    def finish():
        scale = power_box[0]
        for key in [k for k in flight if k[0] in ("mid", "vert")]:
            flight.pop(key).wait_recv()
        for side in range(2):
            own = pl.ds(half_at[side], m)
            dst = pl.ds(pl.multiple_of(half_at[side] - m, m), m)
            for c in range(2):
                base = acc[c, pl.ds(m, rows), own] + came[side][c, pl.ds(m, rows), :]
                ends = jnp.concatenate([vrecv[1, side, c], vrecv[0, side, c]], 0)
                out_obj[c, :, dst] = (base + ends) / scale

    ops = {"rs": rs, "rse": rse, "div": div, "agz": agz, "agp": agp, "agc": agc, "age": age, "corner": corner, "mid": mid, "vert": vert, "power": power, "finish": finish}
    for name, *args in fold_schedule(steps, len(chunks)):
        ops[name](*args)
    assert not flight, flight
    for copy in pending:
        copy.wait_send()


def body(n_gx, n_gy, object_field, probe_field, amplitude, offsets):
    extent = probe_field.shape[-1]
    modes = probe_field.shape[0]
    margin = extent // 2
    rows, cols = object_field.shape[1:]
    positions = amplitude.shape[0]
    ext_shape = (2, rows + 2 * margin + SUB, cols + 2 * margin)
    ext = pl.pallas_call(
        functools.partial(halo_kernel, n_gx, n_gy, margin),
        out_shape=jax.ShapeDtypeStruct(ext_shape, F32),
        in_specs=[HBM],
        out_specs=VMEM,
        scratch_shapes=[pltpu.SemaphoreType.DMA((2, 2 + 8 * STRIPS)), pltpu.SemaphoreType.DMA((1,))],
        compiler_params=pltpu.CompilerParams(collective_id=0, has_side_effects=True, vmem_limit_bytes=LIMIT),
        name="halo",
    )(object_field)

    planes = 2 * modes + 1
    acc, sums = pl.pallas_call(
        functools.partial(update_kernel, margin),
        grid=(positions,),
        out_shape=(
            jax.ShapeDtypeStruct(ext_shape, F32),
            jax.ShapeDtypeStruct((planes, extent, extent), F32),
        ),
        in_specs=[
            pl.BlockSpec(memory_space=pltpu.SMEM),
            VMEM,
            VMEM,
            pl.BlockSpec((1, extent, extent), lambda i: (i, 0, 0)),
            VMEM,
        ],
        out_specs=(VMEM, VMEM),
        scratch_shapes=[
            pltpu.VMEM((2, extent, extent), F32),
            pltpu.VMEM((modes, 2, extent, extent), F32),
            pltpu.VMEM((2 * extent, modes * extent), BF16),
            pltpu.VMEM((modes * extent, 2 * extent), BF16),
            pltpu.VMEM((modes * extent, 2 * extent), F32),
            pltpu.VMEM((2 * extent, 2 * extent), BF16),
            pltpu.VMEM((2 * extent, 2 * extent), BF16),
        ],
        compiler_params=pltpu.CompilerParams(vmem_limit_bytes=LIMIT),
        name="update",
    )(offsets.transpose(1, 2, 0), ext, probe_field, amplitude[:, 0], dft_tables(extent))

    plan = reduce_plan(n_gx, n_gy)
    peers = sum((1 << (cx + cy)) - 1 for _, cx, _, cy in plan)
    chunks = ((0, modes + 1), (modes + 1, planes))
    out_obj, out_probe = pl.pallas_call(
        functools.partial(fold_kernel, n_gx, n_gy, margin, chunks),
        out_shape=(
            jax.ShapeDtypeStruct(object_field.shape, F32),
            jax.ShapeDtypeStruct((2 * modes, extent, extent), F32),
        ),
        in_specs=[VMEM] * 3,
        out_specs=(VMEM, VMEM),
        scratch_shapes=[
            pltpu.VMEM((2, rows + 2 * margin, margin), F32),
            pltpu.VMEM((2, rows + 2 * margin, margin), F32),
            pltpu.VMEM((2, 2, 2, margin, margin), F32),
            pltpu.VMEM((2, 2, 2, margin, margin), F32),
            pltpu.VMEM((len(plan), planes, extent, extent), F32),
            pltpu.VMEM((planes, 3 * extent, extent), F32),
            pltpu.SemaphoreType.DMA((2, 8 * PIECES + 2 * MIDS + (peers + 24) * len(chunks))),
        ],
        compiler_params=pltpu.CompilerParams(
            collective_id=1, has_side_effects=True, vmem_limit_bytes=LIMIT
        ),
        name="fold",
    )(acc, probe_field, sums)
    return object_field + out_obj, probe_field + out_probe.reshape(probe_field.shape)


def solution(mesh):
    in_specs = (P(None, "gx", "gy"), P(), P("gx", "gy", None, None), P("gx", "gy", None))
    out_specs = (P(None, "gx", "gy"), P())
    step = functools.partial(body, mesh.shape["gx"], mesh.shape["gy"])
    return jax.shard_map(step, mesh=mesh, in_specs=in_specs, out_specs=out_specs, check_vma=False)
```

time: 74.7 us -> 68.6 us (0.918)
  Pallas kernels: 70.7 us -> 64.5 us
    pallas_call x1, Pallas kernels: 40.9 us -> 35.1 us  [body(): pl.pallas_call(functools.partial(fold_kernel, n_gx, n_gy, margin, chunks)...]
where the time goes in v2:
time: 68.6 us; the launch traced here: 68.3 us
  Pallas kernels  64.5 us (94%)
  other arithmetic  1.97 us (3%)
  local copies, waits for them, and re-layouts  1.15 us (2%)
  between operations  0.72 us (1%)
    pallas_call x1, Pallas kernels, body(): pl.pallas_call(functools.partial(fold_kernel, n_gx, n_gy, margin, chunks)...  35.1 us
    pallas_call x1, Pallas kernels, body(): pl.pallas_call(functools.partial(halo_kernel, n_gx, n_gy, margin), out_sh...  18.4 us
    pallas_call x1, Pallas kernels, body(): pl.pallas_call(functools.partial(update_kernel, margin), grid=(positions,...  11 us

profile of v2, /device:TPU:0, one launch (start us, length us, event | category | flops | bytes accessed | tf_op | source)
XLA Modules:
  0.0 68.3 jit_solution(9095801161737361651)
XLA Ops:
  0.6 0.0 copy-start
  0.6 0.0 copy-start.1
  0.7 1.1 %copy-done.1 = f32[2,256,256]{2,1,0:T(8,128)S(1)} copy-done((f32[2,256,256]{2,1,0:T(8,128)S(1)}, f32[2,256,256]{2,1,0:T(8,128)}, u32[]{:S(2)}) %copy-start.1) | copy-done | bytes 524312
  1.8 0.0 copy-start.3
  1.8 0.0 copy-start.4
  1.8 0.0 copy-start.5
  1.8 18.4 %halo.1.ext = f32[2,520,512]{2,1,0:T(8,128)S(1)} custom-call(f32[2,256,256]{2,1,0:T(8,128)S(1)} %copy-done.1), custom_call_target="tpu_custom_call" | custom-call | tf_op jit(solution)/shard_map/halo/pallas_call | solution.py:449
  20.2 0.0 copy-done
  20.2 0.0 copy-done.3
  20.2 0.0 copy-done.4
  20.2 0.0 copy-done.5
  20.3 11.0 %update.1 = (f32[2,520,512]{2,1,0:T(8,128)S(1)}, f32[5,256,256]{2,1,0:T(8,128)S(1)}) custom-call(s32[1,2,4]{2,1,0:T(2,128)S(1)} %bitcast.5, f32[2,520,512]{2,1,0:T(8,128)S(1)} %halo.1.ext, f32[2,2,256,256]{3,2,1,0:T(8,128)S(1)} %copy-done, f32[4,256,256]{2,1,0:T(8,128)S(1)} %bitcast.3, bf16[256,512]{1,0:T(8,128)(2,1)S(1)} %copy-done.4), custom_call_target="tpu_custom_call" | custom-call | tf_op jit(solution)/shard_map/update/pallas_call | solution.py:460
  31.2 0.0 copy-start.2
  31.3 35.1 %fold.1 = (f32[2,256,256]{2,1,0:T(8,128)S(1)}, f32[4,256,256]{2,1,0:T(8,128)S(1)}) custom-call(f32[2,520,512]{2,1,0:T(8,128)S(1)} %get-tuple-element.6.acc, f32[2,2,256,256]{3,2,1,0:T(8,128)S(1)} %copy-done, f32[5,256,256]{2,1,0:T(8,128)S(1)} %get-tuple-element.7.sums), custom_call_target="tpu_custom_call" | custom-call | tf_op jit(solution)/shard_map/fold/pallas_call | solution.py:491
  66.4 0.0 copy-done.2
  66.4 0.9 %add.6 = f32[2,256,256]{2,1,0:T(8,128)} add(f32[2,256,256]{2,1,0:T(8,128)S(1)} %copy-done.2, f32[2,256,256]{2,1,0:T(8,128)S(1)} %get-tuple-element.8) | non-fusion elementwise | flops 131072 | bytes 1572864 | tf_op jit(solution)/shard_map/add | solution.py:513
  67.2 1.1 %add.7 = f32[2,2,256,256]{3,2,1,0:T(8,128)} add(f32[2,2,256,256]{3,2,1,0:T(8,128)S(1)} %copy-done, f32[2,2,256,256]{3,2,1,0:T(8,128)S(1)} %bitcast.4) | non-fusion elementwise | flops 262144 | bytes 3145728 | tf_op jit(solution)/shard_map/add | solution.py:513
Async XLA Ops:
  0.6 19.6 %copy-start = (f32[2,2,256,256]{3,2,1,0:T(8,128)S(1)}, f32[2,2,256,256]{3,2,1,0:T(8,128)}, u32[]{:S(2)}) copy-start(f32[2,2,256,256]{3,2,1,0:T(8,128)} %probe.3) | copy-start | bytes 3145732
  0.6 1.1 %copy-start.1 = (f32[2,256,256]{2,1,0:T(8,128)S(1)}, f32[2,256,256]{2,1,0:T(8,128)}, u32[]{:S(2)}) copy-start(f32[2,256,256]{2,1,0:T(8,128)} %obj.1) | copy-start | bytes 1572868
  1.8 18.5 %copy-start.3 = (f32[4,1,256,256]{3,2,1,0:T(8,128)S(1)}, f32[4,1,256,256]{3,2,1,0:T(8,128)}, u32[]{:S(2)}) copy-start(f32[4,1,256,256]{3,2,1,0:T(8,128)} %param.7) | copy-start | bytes 3145732
  1.8 18.5 %copy-start.4 = (bf16[256,512]{1,0:T(8,128)(2,1)S(1)}, bf16[256,512]{1,0:T(8,128)(2,1)}, u32[]{:S(2)}) copy-start(bf16[256,512]{1,0:T(8,128)(2,1)} %constant.2.clone.table) | copy-start | bytes 786436
  1.8 18.5 %copy-start.5 = (s32[4,1,2]{0,2,1:T(2,128)S(1)}, s32[4,1,2]{0,2,1:T(2,128)}, u32[]{:S(2)}) copy-start(s32[4,1,2]{0,2,1:T(2,128)} %param.8) | copy-start | bytes 100
  31.2 35.1 %copy-start.2 = (f32[2,256,256]{2,1,0:T(8,128)S(1)}, f32[2,256,256]{2,1,0:T(8,128)}, u32[]{:S(2)}) copy-start(f32[2,256,256]{2,1,0:T(8,128)} %obj.1) | copy-start | bytes 1572868

commit v3 on v2

--- a/solution.py
+++ b/solution.py
@@ -16,6 +16,7 @@
 BF16 = jnp.bfloat16
 CHUNK = 32
 SUB = 8
+LANE = 128
 STRIPS = 2
 PIECES = 2
 MIDS = 2
@@ -52,6 +53,7 @@
     gx, gy = lax.axis_index("gx"), lax.axis_index("gy")
     rows, cols = obj.shape[1], obj.shape[2]
     m = margin
+    mt, ct = m // LANE, cols // LANE
     odd = lax.rem(gy, 2)
     up = (lax.rem(gx + n_gx - 1, n_gx), gy)
     down = (lax.rem(gx + 1, n_gx), gy)
@@ -59,10 +61,16 @@
     near = (gx, gy + step_y)
     far = (gx, lax.rem(gy - step_y + n_gy, n_gy))
     sides = (near, far)
-    half_at = (pl.multiple_of((1 - odd) * (cols - m), m), pl.multiple_of(odd * (cols - m), m))
-    lands_at = (pl.multiple_of(odd * (m + cols), m), pl.multiple_of((1 - odd) * (m + cols), m))
-    own = pltpu.make_async_copy(obj, ext.at[:, pl.ds(m, rows), pl.ds(m, cols)], local_sem.at[0])
-    own.start()
+    half_at = ((1 - odd) * (ct - mt), odd * (ct - mt))
+    lands_at = (odd * (mt + ct), (1 - odd) * (mt + ct))
+    owns = [
+        pltpu.make_async_copy(
+            obj.at[:, :, pl.ds(t * LANE, LANE)], ext.at[:, mt + t, pl.ds(m, rows), :], local_sem.at[t]
+        )
+        for t in range(ct)
+    ]
+    for own in owns:
+        own.start()
     greet((up, down, near, far))
     slot = [0]
     pending = []
@@ -79,139 +87,169 @@
     arrivals = []
     waits = []
 
+    def lanes(side, t):
+        return pl.ds(pl.multiple_of((half_at[side] + t) * LANE, LANE), LANE)
+
     def middle(side):
-        src = obj.at[:, :, pl.ds(half_at[side], m)]
-        dst = ext.at[:, pl.ds(m, rows), pl.ds(lands_at[side], m)]
-        waits.append(send(src, dst, sides[side]))
+        for t in range(mt):
+            dst = ext.at[:, lands_at[side] + t, pl.ds(m, rows), :]
+            waits.append(send(obj.at[:, :, lanes(side, t)], dst, sides[side]))
 
     def vertical(side):
         for i in range(STRIPS):
             for src_row, dst_row, device in ways:
                 band = pl.ds(dst_row + i * piece, piece)
-                src = obj.at[:, pl.ds(src_row + i * piece, piece), pl.ds(half_at[side], m)]
-                dst = ext.at[:, band, pl.ds(m + half_at[side], m)]
-                arrivals.append((send(src, dst, device), side, band))
+                for t in range(mt):
+                    src = obj.at[:, pl.ds(src_row + i * piece, piece), lanes(side, t)]
+                    dst = ext.at[:, mt + half_at[side] + t, band, :]
+                    arrivals.append((send(src, dst, device), side, band, t))
 
     vertical(1)
     middle(1)
     vertical(0)
     middle(0)
-    for copy, side, band in arrivals:
+    for copy, side, band, t in arrivals:
         copy.wait_recv()
-        src = ext.at[:, band, pl.ds(m + half_at[side], m)]
-        waits.append(send(src, ext.at[:, band, pl.ds(lands_at[side], m)], sides[side]))
+        src = ext.at[:, mt + half_at[side] + t, band, :]
+        waits.append(send(src, ext.at[:, lands_at[side] + t, band, :], sides[side]))
     for copy in waits:
         copy.wait_recv()
     for copy in pending:
         copy.wait_send()
-    own.wait()
-
-
-def update_kernel(
-    margin, offs, ext, probe, amp, table, acc, sums, win, psi, xbuf, ybuf, far, fr, frt
-):
-    p = pl.program_id(0)
+    for own in owns:
+        own.wait()
+
+
+def update_kernel(margin, offs, ext, probe, amp, table, acc, sums, win, psi, xbuf, ybuf, far, fr, frt):
+    positions = amp.shape[0]
     extent = probe.shape[-1]
     modes = probe.shape[0]
-    width = ext.shape[2]
-    r0 = offs[0, 0, p] + margin
-    c0 = offs[0, 1, p] + margin
-    back_shift = lax.rem(width - c0, width)
-    low = lax.rem(r0, SUB)
-    base = r0 - low
-    tall = CHUNK + SUB
-    row_shift = lax.rem(tall - low, tall)
-    n_chunks = extent // CHUNK
-
-    @pl.when(p == 0)
-    def _():
-        acc[...] = jnp.zeros_like(acc)
-        sums[...] = jnp.zeros_like(sums)
-        c, s = table[:, :extent], table[:, extent:]
-        fr[:extent, :extent] = c
-        fr[:extent, extent:] = s
-        fr[extent:, :extent] = -s
-        fr[extent:, extent:] = c
-        frt[:extent, :extent] = c
-        frt[:extent, extent:] = -s
-        frt[extent:, :extent] = s
-        frt[extent:, extent:] = c
-
-    @pl.loop(0, n_chunks, unroll=8)
-    def _(i):
-        rb = pl.multiple_of(i * CHUNK, CHUNK)
+    last = ext.shape[1] - extent // LANE - 1
+    starts = range(0, extent, CHUNK)
+
+    c, s = table[:, :extent], table[:, extent:]
+    fr[:extent, :extent] = c
+    fr[:extent, extent:] = s
+    fr[extent:, :extent] = -s
+    fr[extent:, extent:] = c
+    frt[:extent, :extent] = c
+    frt[:extent, extent:] = -s
+    frt[extent:, :extent] = s
+    frt[extent:, extent:] = c
+
+    lane = lax.broadcasted_iota(jnp.int32, (CHUNK, LANE), 1)
+
+    def place(p):
+        c0 = offs[0, 1, p] + margin
+        tile = jnp.minimum(c0 // LANE, last)
+        return offs[0, 0, p] + margin, tile, c0 - tile * LANE
+
+    def add(plane, here, value, p):
+        if p == 0:
+            sums[plane, here, :] = value
+        else:
+            sums[plane, here, :] += value
+
+    def extract(p, rb):
+        r0, tile, low = place(p)
         here = pl.ds(rb, CHUNK)
+        q = p % 2
         w = []
         for part in range(2):
-            line = ext[part, pl.ds(pl.multiple_of(base + rb, SUB), tall), :]
-            line = pltpu.roll(line, row_shift, 0)[:CHUNK]
-            w.append(pltpu.roll(line, back_shift, 1)[:, :extent])
-            win[part, here, :] = w[part]
-        sums[0, here, :] += w[0] * w[0] + w[1] * w[1]
+            line = [
+                pltpu.roll(ext[part, tile + t, pl.ds(r0 + rb, CHUNK), :], lax.rem(LANE - low, LANE), 1)
+                for t in range(extent // LANE + 1)
+            ]
+            line = [jnp.where(lane < LANE - low, a, b) for a, b in zip(line, line[1:])]
+            w.append(jnp.concatenate(line, 1))
+            win[q, part, here, :] = w[part]
+        add(0, here, w[0] * w[0] + w[1] * w[1], p)
         for k in range(modes):
             cols = slice(k * extent, (k + 1) * extent)
             pr, pi = probe[k, 0, here, :], probe[k, 1, here, :]
             psi_re = pr * w[0] - pi * w[1]
             psi_im = pr * w[1] + pi * w[0]
-            psi[k, 0, here, :] = psi_re
-            psi[k, 1, here, :] = psi_im
-            xbuf[here, cols] = psi_re.astype(BF16)
-            xbuf[pl.ds(extent + rb, CHUNK), cols] = psi_im.astype(BF16)
-
-    def rows_then_cols(row_table, col_table):
-        for part in range(2):
-            table = row_table[part * extent : (part + 1) * extent, :]
-            out = jnp.dot(table, xbuf[...], preferred_element_type=F32).astype(BF16)
-            for k in range(modes):
-                ybuf[k * extent : (k + 1) * extent, part * extent : (part + 1) * extent] = out[
-                    :, k * extent : (k + 1) * extent
-                ]
+            psi[q, k, 0, here, :] = psi_re
+            psi[q, k, 1, here, :] = psi_im
+            xbuf[q, here, cols] = psi_re.astype(BF16)
+            xbuf[q, pl.ds(extent + rb, CHUNK), cols] = psi_im.astype(BF16)
+
+    def rows_pass(q, row_table, part):
+        band = row_table[part * extent : (part + 1) * extent, :]
+        out = jnp.dot(band, xbuf[q], preferred_element_type=F32).astype(BF16)
         for k in range(modes):
-            band = slice(k * extent, (k + 1) * extent)
-            far[band, :] = jnp.dot(ybuf[band, :], col_table[...], preferred_element_type=F32)
-
-    rows_then_cols(fr, frt)
-
-    @pl.loop(0, n_chunks, unroll=8)
-    def _(i):
-        rb = pl.multiple_of(i * CHUNK, CHUNK)
+            ybuf[k * extent : (k + 1) * extent, part * extent : (part + 1) * extent] = out[
+                :, k * extent : (k + 1) * extent
+            ]
+
+    def cols_pass(q, col_table, k):
+        band = slice(k * extent, (k + 1) * extent)
+        far[q, band, :] = jnp.dot(ybuf[band, :], col_table[...], preferred_element_type=F32)
+
+    def project(p, rb):
+        q = p % 2
         parts = []
         intensity = jnp.zeros((CHUNK, extent), F32)
         for k in range(modes):
             at = pl.ds(k * extent + rb, CHUNK)
-            re, im = far[at, :extent], far[at, extent:]
+            re, im = far[q, at, :extent], far[q, at, extent:]
             intensity += re * re + im * im
             parts.append((re, im))
-        factor = amp[0, pl.ds(rb, CHUNK), :] * jnp.minimum(lax.rsqrt(intensity), 4.0)
+        factor = amp[p, pl.ds(rb, CHUNK), :] * jnp.minimum(lax.rsqrt(intensity), 4.0)
         for k in range(modes):
             cols = slice(k * extent, (k + 1) * extent)
-            xbuf[pl.ds(rb, CHUNK), cols] = (parts[k][0] * factor).astype(BF16)
-            xbuf[pl.ds(extent + rb, CHUNK), cols] = (parts[k][1] * factor).astype(BF16)
-
-    rows_then_cols(frt, fr)
-
-    @pl.loop(0, n_chunks, unroll=8)
-    def _(i):
-        rb = pl.multiple_of(i * CHUNK, CHUNK)
+            xbuf[q, pl.ds(rb, CHUNK), cols] = (parts[k][0] * factor).astype(BF16)
+            xbuf[q, pl.ds(extent + rb, CHUNK), cols] = (parts[k][1] * factor).astype(BF16)
+
+    def correct(p, rb):
+        r0, tile, low = place(p)
+        q = p % 2
         here = pl.ds(rb, CHUNK)
-        wr, wi = win[0, here, :], win[1, here, :]
+        wr, wi = win[q, 0, here, :], win[q, 1, here, :]
         obj_re = jnp.zeros((CHUNK, extent), F32)
         obj_im = jnp.zeros((CHUNK, extent), F32)
         for k in range(modes):
             at = pl.ds(k * extent + rb, CHUNK)
-            dr = far[at, :extent] - psi[k, 0, here, :]
-            di = far[at, extent:] - psi[k, 1, here, :]
+            dr = far[q, at, :extent] - psi[q, k, 0, here, :]
+            di = far[q, at, extent:] - psi[q, k, 1, here, :]
             pr, pi = probe[k, 0, here, :], probe[k, 1, here, :]
             obj_re += pr * dr + pi * di
             obj_im += pr * di - pi * dr
-            sums[2 * k + 1, here, :] += wr * dr + wi * di
-            sums[2 * k + 2, here, :] += wr * di - wi * dr
-        blank = jnp.zeros((CHUNK, width - extent), F32)
-        below = jnp.zeros((SUB, width), F32)
+            add(2 * k + 1, here, wr * dr + wi * di, p)
+            add(2 * k + 2, here, wr * di - wi * dr, p)
+        blank = jnp.zeros((CHUNK, LANE), F32)
         for part, value in enumerate((obj_re, obj_im)):
-            line = pltpu.roll(jnp.concatenate([value, blank], 1), lax.rem(c0, width), 1)
-            line = pltpu.roll(jnp.concatenate([line, below], 0), low, 0)
-            acc[part, pl.ds(pl.multiple_of(base + rb, SUB), tall), :] += line
+            line = [
+                pltpu.roll(value[:, t * LANE : (t + 1) * LANE], lax.rem(low, LANE), 1)
+                for t in range(extent // LANE)
+            ]
+            for t, (a, b) in enumerate(zip([blank] + line, line + [blank])):
+                acc[part, tile + t, pl.ds(r0 + rb, CHUNK), :] += jnp.where(lane < low, a, b)
+
+    def clear(part, t):
+        acc[part, t] = jnp.zeros(acc.shape[2:], F32)
+
+    def beside(matmuls, others):
+        n = len(matmuls)
+        for i, (call, args) in enumerate(matmuls):
+            call(*args)
+            for other, rest in others[i * len(others) // n : (i + 1) * len(others) // n]:
+                other(*rest)
+
+    for rb in starts:
+        extract(0, rb)
+    for p in range(positions):
+        q = p % 2
+        there = [(rows_pass, (q, fr, 0)), (rows_pass, (q, fr, 1))]
+        there += [(cols_pass, (q, frt, k)) for k in range(modes)]
+        back = [(rows_pass, (q, frt, 0)), (rows_pass, (q, frt, 1))]
+        back += [(cols_pass, (q, fr, k)) for k in range(modes)]
+        beside(there, [(correct, (p - 1, rb)) for rb in starts] if p else [(clear, (i, t)) for i in range(2) for t in range(acc.shape[1])])
+        for rb in starts:
+            project(p, rb)
+        beside(back, [(extract, (p + 1, rb)) for rb in starts] if p + 1 < positions else [])
+    for rb in starts:
+        correct(positions - 1, rb)
 
 
 def reduce_plan(n_gx, n_gy):
@@ -255,6 +293,7 @@
     planes, extent = sums.shape[0], sums.shape[1]
     modes = probe.shape[0]
     m = margin
+    mt, ct = m // LANE, cols // LANE
     odd = lax.rem(gy, 2)
     up = (lax.rem(gx + n_gx - 1, n_gx), gy)
     down = (lax.rem(gx + 1, n_gx), gy)
@@ -263,8 +302,8 @@
     far = (gx, lax.rem(gy - step_y + n_gy, n_gy))
     sides = (near, far)
     came = (from_near, from_far)
-    halo_at = (pl.multiple_of((1 - odd) * (m + cols), m), pl.multiple_of(odd * (m + cols), m))
-    half_at = (pl.multiple_of(m + (1 - odd) * (cols - m), m), pl.multiple_of(m + odd * (cols - m), m))
+    halo_at = ((1 - odd) * (mt + ct), odd * (mt + ct))
+    half_at = (mt + (1 - odd) * (ct - mt), mt + odd * (ct - mt))
     plan = reduce_plan(n_gx, n_gy)
     steps = len(plan)
 
@@ -398,18 +437,25 @@
 
     def corner(side, b, i):
         band = pl.ds(band_at[b] + i * piece, piece)
-        flight["corner", side, b, i] = send(acc.at[:, band, pl.ds(halo_at[side], m)], came[side].at[:, band, :], sides[side])
+        flight["corner", side, b, i] = send(
+            acc.at[:, pl.ds(halo_at[side], mt), band, :], came[side].at[:, :, band, :], sides[side]
+        )
 
     def mid(side, i, of):
         band = pl.ds(m + i * (rows // of), rows // of)
-        flight["mid", side, i] = send(acc.at[:, band, pl.ds(halo_at[side], m)], came[side].at[:, band, :], sides[side])
+        flight["mid", side, i] = send(
+            acc.at[:, pl.ds(halo_at[side], mt), band, :], came[side].at[:, :, band, :], sides[side]
+        )
 
     def vert(side, b, i):
         flight.pop(("corner", side, b, i)).wait_recv()
         band = pl.ds(band_at[b] + i * piece, piece)
         here = pl.ds(i * piece, piece)
-        vsend[b, side, :, here, :] = acc[:, band, pl.ds(half_at[side], m)] + came[side][:, band, :]
-        flight["vert", side, b, i] = send(vsend.at[b, side, :, here, :], vrecv.at[b, side, :, here, :], (up, down)[b])
+        own = acc[:, pl.ds(half_at[side], mt), band, :]
+        vsend[b, side, :, :, here, :] = own + came[side][:, :, band, :]
+        flight["vert", side, b, i] = send(
+            vsend.at[b, side, :, :, here, :], vrecv.at[b, side, :, :, here, :], (up, down)[b]
+        )
 
     power_box = []
     def power():
@@ -424,12 +470,12 @@
         for key in [k for k in flight if k[0] in ("mid", "vert")]:
             flight.pop(key).wait_recv()
         for side in range(2):
-            own = pl.ds(half_at[side], m)
-            dst = pl.ds(pl.multiple_of(half_at[side] - m, m), m)
-            for c in range(2):
-                base = acc[c, pl.ds(m, rows), own] + came[side][c, pl.ds(m, rows), :]
-                ends = jnp.concatenate([vrecv[1, side, c], vrecv[0, side, c]], 0)
-                out_obj[c, :, dst] = (base + ends) / scale
+            for t in range(mt):
+                dst = pl.ds(pl.multiple_of((half_at[side] - mt + t) * LANE, LANE), LANE)
+                for c in range(2):
+                    base = acc[c, half_at[side] + t, pl.ds(m, rows), :] + came[side][c, t, pl.ds(m, rows), :]
+                    ends = jnp.concatenate([vrecv[1, side, c, t], vrecv[0, side, c, t]], 0)
+                    out_obj[c, :, dst] = (base + ends) / scale
 
     ops = {"rs": rs, "rse": rse, "div": div, "agz": agz, "agp": agp, "agc": agc, "age": age, "corner": corner, "mid": mid, "vert": vert, "power": power, "finish": finish}
     for name, *args in fold_schedule(steps, len(chunks)):
@@ -444,14 +490,14 @@
     modes = probe_field.shape[0]
     margin = extent // 2
     rows, cols = object_field.shape[1:]
-    positions = amplitude.shape[0]
-    ext_shape = (2, rows + 2 * margin + SUB, cols + 2 * margin)
+    mt, ct = margin // LANE, cols // LANE
+    ext_shape = (2, 2 * mt + ct, rows + 2 * margin, LANE)
     ext = pl.pallas_call(
         functools.partial(halo_kernel, n_gx, n_gy, margin),
         out_shape=jax.ShapeDtypeStruct(ext_shape, F32),
         in_specs=[HBM],
         out_specs=VMEM,
-        scratch_shapes=[pltpu.SemaphoreType.DMA((2, 2 + 8 * STRIPS)), pltpu.SemaphoreType.DMA((1,))],
+        scratch_shapes=[pltpu.SemaphoreType.DMA((2, (2 + 8 * STRIPS) * mt)), pltpu.SemaphoreType.DMA((ct,))],
         compiler_params=pltpu.CompilerParams(collective_id=0, has_side_effects=True, vmem_limit_bytes=LIMIT),
         name="halo",
     )(object_field)
@@ -459,7 +505,6 @@
     planes = 2 * modes + 1
     acc, sums = pl.pallas_call(
         functools.partial(update_kernel, margin),
-        grid=(positions,),
         out_shape=(
             jax.ShapeDtypeStruct(ext_shape, F32),
             jax.ShapeDtypeStruct((planes, extent, extent), F32),
@@ -468,16 +513,16 @@
             pl.BlockSpec(memory_space=pltpu.SMEM),
             VMEM,
             VMEM,
-            pl.BlockSpec((1, extent, extent), lambda i: (i, 0, 0)),
+            VMEM,
             VMEM,
         ],
         out_specs=(VMEM, VMEM),
         scratch_shapes=[
-            pltpu.VMEM((2, extent, extent), F32),
-            pltpu.VMEM((modes, 2, extent, extent), F32),
-            pltpu.VMEM((2 * extent, modes * extent), BF16),
+            pltpu.VMEM((2, 2, extent, extent), F32),
+            pltpu.VMEM((2, modes, 2, extent, extent), F32),
+            pltpu.VMEM((2, 2 * extent, modes * extent), BF16),
             pltpu.VMEM((modes * extent, 2 * extent), BF16),
-            pltpu.VMEM((modes * extent, 2 * extent), F32),
+            pltpu.VMEM((2, modes * extent, 2 * extent), F32),
             pltpu.VMEM((2 * extent, 2 * extent), BF16),
             pltpu.VMEM((2 * extent, 2 * extent), BF16),
         ],
@@ -497,10 +542,10 @@
         in_specs=[VMEM] * 3,
         out_specs=(VMEM, VMEM),
         scratch_shapes=[
-            pltpu.VMEM((2, rows + 2 * margin, margin), F32),
-            pltpu.VMEM((2, rows + 2 * margin, margin), F32),
-            pltpu.VMEM((2, 2, 2, margin, margin), F32),
-            pltpu.VMEM((2, 2, 2, margin, margin), F32),
+            pltpu.VMEM((2, mt, rows + 2 * margin, LANE), F32),
+            pltpu.VMEM((2, mt, rows + 2 * margin, LANE), F32),
+            pltpu.VMEM((2, 2, 2, mt, margin, LANE), F32),
+            pltpu.VMEM((2, 2, 2, mt, margin, LANE), F32),
             pltpu.VMEM((len(plan), planes, extent, extent), F32),
             pltpu.VMEM((planes, 3 * extent, extent), F32),
             pltpu.SemaphoreType.DMA((2, 8 * PIECES + 2 * MIDS + (peers + 24) * len(chunks))),

time: 68.6 us -> 65.3 us (0.952)
  Pallas kernels: 64.5 us -> 61.3 us
    pallas_call x1, Pallas kernels: 11 us -> 7.71 us  [body(): pl.pallas_call(functools.partial(update_kernel, margin), out_shape=(jax.S...]
where the time goes in v3:
time: 65.3 us; the launch traced here: 65.1 us
  Pallas kernels  61.3 us (94%)
  other arithmetic  1.97 us (3%)
  local copies, waits for them, and re-layouts  1.14 us (2%)
  between operations  0.7 us (1%)
    pallas_call x1, Pallas kernels, body(): pl.pallas_call(functools.partial(fold_kernel, n_gx, n_gy, margin, chunks)...  35.1 us
    pallas_call x1, Pallas kernels, body(): pl.pallas_call(functools.partial(halo_kernel, n_gx, n_gy, margin), out_sh...  18.4 us
    pallas_call x1, Pallas kernels, body(): pl.pallas_call(functools.partial(update_kernel, margin), out_shape=(jax.S...  7.71 us

profile of v3, /device:TPU:0, one launch (start us, length us, event | category | flops | bytes accessed | tf_op | source)
XLA Modules:
  0.0 65.1 jit_solution(14261167791929773268)
XLA Ops:
  0.6 0.0 copy-start
  0.6 0.0 copy-start.1
  0.7 1.1 %copy-done.1 = f32[2,256,256]{2,1,0:T(8,128)S(1)} copy-done((f32[2,256,256]{2,1,0:T(8,128)S(1)}, f32[2,256,256]{2,1,0:T(8,128)}, u32[]{:S(2)}) %copy-start.1) | copy-done | bytes 524312
  1.8 0.0 copy-start.2
  1.8 0.0 copy-start.3
  1.8 0.0 copy-start.4
  1.8 18.4 %halo.1.ext = f32[2,4,512,128]{3,2,1,0:T(8,128)S(1)} custom-call(f32[2,256,256]{2,1,0:T(8,128)S(1)} %copy-done.1), custom_call_target="tpu_custom_call" | custom-call | tf_op jit(solution)/shard_map/halo/pallas_call | solution.py:495
  20.2 0.0 copy-done
  20.2 0.0 copy-done.2
  20.2 0.0 copy-done.3
  20.2 0.0 copy-done.4
  20.2 7.7 %update.1 = (f32[2,4,512,128]{3,2,1,0:T(8,128)S(1)}, f32[5,256,256]{2,1,0:T(8,128)S(1)}) custom-call(s32[1,2,4]{2,1,0:T(2,128)S(1)} %bitcast.5, f32[2,4,512,128]{3,2,1,0:T(8,128)S(1)} %halo.1.ext, f32[2,2,256,256]{3,2,1,0:T(8,128)S(1)} %copy-done, f32[4,256,256]{2,1,0:T(8,128)S(1)} %bitcast.3, bf16[256,512]{1,0:T(8,128)(2,1)S(1)} %copy-done.3), custom_call_target="tpu_custom_call" | custom-call | tf_op jit(solution)/shard_map/update/pallas_call | solution.py:506
  28.0 35.1 %fold.1 = (f32[2,256,256]{2,1,0:T(8,128)S(1)}, f32[4,256,256]{2,1,0:T(8,128)S(1)}) custom-call(f32[2,4,512,128]{3,2,1,0:T(8,128)S(1)} %get-tuple-element.6.acc, f32[2,2,256,256]{3,2,1,0:T(8,128)S(1)} %copy-done, f32[5,256,256]{2,1,0:T(8,128)S(1)} %get-tuple-element.7.sums), custom_call_target="tpu_custom_call" | custom-call | tf_op jit(solution)/shard_map/fold/pallas_call | solution.py:536
  63.1 0.9 %add.6 = f32[2,256,256]{2,1,0:T(8,128)} add(f32[2,256,256]{2,1,0:T(8,128)S(1)} %copy-done.1, f32[2,256,256]{2,1,0:T(8,128)S(1)} %get-tuple-element.8) | non-fusion elementwise | flops 131072 | bytes 1572864 | tf_op jit(solution)/shard_map/add | solution.py:558
  64.0 1.1 %add.7 = f32[2,2,256,256]{3,2,1,0:T(8,128)} add(f32[2,2,256,256]{3,2,1,0:T(8,128)S(1)} %copy-done, f32[2,2,256,256]{3,2,1,0:T(8,128)S(1)} %bitcast.4) | non-fusion elementwise | flops 262144 | bytes 3145728 | tf_op jit(solution)/shard_map/add | solution.py:558
Async XLA Ops:
  0.6 19.6 %copy-start = (f32[2,2,256,256]{3,2,1,0:T(8,128)S(1)}, f32[2,2,256,256]{3,2,1,0:T(8,128)}, u32[]{:S(2)}) copy-start(f32[2,2,256,256]{3,2,1,0:T(8,128)} %probe.3) | copy-start | bytes 3145732
  0.6 1.1 %copy-start.1 = (f32[2,256,256]{2,1,0:T(8,128)S(1)}, f32[2,256,256]{2,1,0:T(8,128)}, u32[]{:S(2)}) copy-start(f32[2,256,256]{2,1,0:T(8,128)} %obj.1) | copy-start | bytes 1572868
  1.8 18.4 %copy-start.2 = (f32[4,1,256,256]{3,2,1,0:T(8,128)S(1)}, f32[4,1,256,256]{3,2,1,0:T(8,128)}, u32[]{:S(2)}) copy-start(f32[4,1,256,256]{3,2,1,0:T(8,128)} %param.7) | copy-start | bytes 3145732
  1.8 18.5 %copy-start.3 = (bf16[256,512]{1,0:T(8,128)(2,1)S(1)}, bf16[256,512]{1,0:T(8,128)(2,1)}, u32[]{:S(2)}) copy-start(bf16[256,512]{1,0:T(8,128)(2,1)} %constant.2.clone.table) | copy-start | bytes 786436
  1.8 18.5 %copy-start.4 = (s32[4,1,2]{0,2,1:T(2,128)S(1)}, s32[4,1,2]{0,2,1:T(2,128)}, u32[]{:S(2)}) copy-start(s32[4,1,2]{0,2,1:T(2,128)} %param.8) | copy-start | bytes 100

commit v4 on v3

--- a/solution.py
+++ b/solution.py
@@ -20,7 +20,8 @@
 STRIPS = 2
 PIECES = 2
 MIDS = 2
-LIMIT = 30 << 20
+LIMIT = 8 << 20
+STEP_LIMIT = 40 << 20
 
 
 def dft_tables(extent):
@@ -120,138 +121,6 @@
         own.wait()
 
 
-def update_kernel(margin, offs, ext, probe, amp, table, acc, sums, win, psi, xbuf, ybuf, far, fr, frt):
-    positions = amp.shape[0]
-    extent = probe.shape[-1]
-    modes = probe.shape[0]
-    last = ext.shape[1] - extent // LANE - 1
-    starts = range(0, extent, CHUNK)
-
-    c, s = table[:, :extent], table[:, extent:]
-    fr[:extent, :extent] = c
-    fr[:extent, extent:] = s
-    fr[extent:, :extent] = -s
-    fr[extent:, extent:] = c
-    frt[:extent, :extent] = c
-    frt[:extent, extent:] = -s
-    frt[extent:, :extent] = s
-    frt[extent:, extent:] = c
-
-    lane = lax.broadcasted_iota(jnp.int32, (CHUNK, LANE), 1)
-
-    def place(p):
-        c0 = offs[0, 1, p] + margin
-        tile = jnp.minimum(c0 // LANE, last)
-        return offs[0, 0, p] + margin, tile, c0 - tile * LANE
-
-    def add(plane, here, value, p):
-        if p == 0:
-            sums[plane, here, :] = value
-        else:
-            sums[plane, here, :] += value
-
-    def extract(p, rb):
-        r0, tile, low = place(p)
-        here = pl.ds(rb, CHUNK)
-        q = p % 2
-        w = []
-        for part in range(2):
-            line = [
-                pltpu.roll(ext[part, tile + t, pl.ds(r0 + rb, CHUNK), :], lax.rem(LANE - low, LANE), 1)
-                for t in range(extent // LANE + 1)
-            ]
-            line = [jnp.where(lane < LANE - low, a, b) for a, b in zip(line, line[1:])]
-            w.append(jnp.concatenate(line, 1))
-            win[q, part, here, :] = w[part]
-        add(0, here, w[0] * w[0] + w[1] * w[1], p)
-        for k in range(modes):
-            cols = slice(k * extent, (k + 1) * extent)
-            pr, pi = probe[k, 0, here, :], probe[k, 1, here, :]
-            psi_re = pr * w[0] - pi * w[1]
-            psi_im = pr * w[1] + pi * w[0]
-            psi[q, k, 0, here, :] = psi_re
-            psi[q, k, 1, here, :] = psi_im
-            xbuf[q, here, cols] = psi_re.astype(BF16)
-            xbuf[q, pl.ds(extent + rb, CHUNK), cols] = psi_im.astype(BF16)
-
-    def rows_pass(q, row_table, part):
-        band = row_table[part * extent : (part + 1) * extent, :]
-        out = jnp.dot(band, xbuf[q], preferred_element_type=F32).astype(BF16)
-        for k in range(modes):
-            ybuf[k * extent : (k + 1) * extent, part * extent : (part + 1) * extent] = out[
-                :, k * extent : (k + 1) * extent
-            ]
-
-    def cols_pass(q, col_table, k):
-        band = slice(k * extent, (k + 1) * extent)
-        far[q, band, :] = jnp.dot(ybuf[band, :], col_table[...], preferred_element_type=F32)
-
-    def project(p, rb):
-        q = p % 2
-        parts = []
-        intensity = jnp.zeros((CHUNK, extent), F32)
-        for k in range(modes):
-            at = pl.ds(k * extent + rb, CHUNK)
-            re, im = far[q, at, :extent], far[q, at, extent:]
-            intensity += re * re + im * im
-            parts.append((re, im))
-        factor = amp[p, pl.ds(rb, CHUNK), :] * jnp.minimum(lax.rsqrt(intensity), 4.0)
-        for k in range(modes):
-            cols = slice(k * extent, (k + 1) * extent)
-            xbuf[q, pl.ds(rb, CHUNK), cols] = (parts[k][0] * factor).astype(BF16)
-            xbuf[q, pl.ds(extent + rb, CHUNK), cols] = (parts[k][1] * factor).astype(BF16)
-
-    def correct(p, rb):
-        r0, tile, low = place(p)
-        q = p % 2
-        here = pl.ds(rb, CHUNK)
-        wr, wi = win[q, 0, here, :], win[q, 1, here, :]
-        obj_re = jnp.zeros((CHUNK, extent), F32)
-        obj_im = jnp.zeros((CHUNK, extent), F32)
-        for k in range(modes):
-            at = pl.ds(k * extent + rb, CHUNK)
-            dr = far[q, at, :extent] - psi[q, k, 0, here, :]
-            di = far[q, at, extent:] - psi[q, k, 1, here, :]
-            pr, pi = probe[k, 0, here, :], probe[k, 1, here, :]
-            obj_re += pr * dr + pi * di
-            obj_im += pr * di - pi * dr
-            add(2 * k + 1, here, wr * dr + wi * di, p)
-            add(2 * k + 2, here, wr * di - wi * dr, p)
-        blank = jnp.zeros((CHUNK, LANE), F32)
-        for part, value in enumerate((obj_re, obj_im)):
-            line = [
-                pltpu.roll(value[:, t * LANE : (t + 1) * LANE], lax.rem(low, LANE), 1)
-                for t in range(extent // LANE)
-            ]
-            for t, (a, b) in enumerate(zip([blank] + line, line + [blank])):
-                acc[part, tile + t, pl.ds(r0 + rb, CHUNK), :] += jnp.where(lane < low, a, b)
-
-    def clear(part, t):
-        acc[part, t] = jnp.zeros(acc.shape[2:], F32)
-
-    def beside(matmuls, others):
-        n = len(matmuls)
-        for i, (call, args) in enumerate(matmuls):
-            call(*args)
-            for other, rest in others[i * len(others) // n : (i + 1) * len(others) // n]:
-                other(*rest)
-
-    for rb in starts:
-        extract(0, rb)
-    for p in range(positions):
-        q = p % 2
-        there = [(rows_pass, (q, fr, 0)), (rows_pass, (q, fr, 1))]
-        there += [(cols_pass, (q, frt, k)) for k in range(modes)]
-        back = [(rows_pass, (q, frt, 0)), (rows_pass, (q, frt, 1))]
-        back += [(cols_pass, (q, fr, k)) for k in range(modes)]
-        beside(there, [(correct, (p - 1, rb)) for rb in starts] if p else [(clear, (i, t)) for i in range(2) for t in range(acc.shape[1])])
-        for rb in starts:
-            project(p, rb)
-        beside(back, [(extract, (p + 1, rb)) for rb in starts] if p + 1 < positions else [])
-    for rb in starts:
-        correct(positions - 1, rb)
-
-
 def reduce_plan(n_gx, n_gy):
     x_bits, y_bits = n_gx.bit_length() - 1, n_gy.bit_length() - 1
     steps = [(0, 0, 0, 1), (0, 1, 1, 1)]
@@ -263,31 +132,10 @@
     return steps
 
 
-def fold_schedule(steps, n):
-    bands = [(b, i) for i in range(PIECES) for b in (0, 1)]
-    near_bands = [("vert", 0, b, i) for b, i in bands]
-    far_bands = [("vert", 1, b, i) for b, i in bands]
-    half = len(far_bands) // 2
-    acts = [("rs", 0, c) for c in range(n)]
-    acts += [("corner", 0, b, i) for b, i in bands] + [("power",)]
-    for c in range(n):
-        acts += [("rse", 0, c), ("rs", 1, c)]
-    acts += [("corner", 1, b, i) for b, i in bands] + near_bands
-    for c in range(n):
-        acts += [("rse", 1, c), ("rs", 2, c)]
-    acts += [("mid", side, i, MIDS) for side in (1, 0) for i in range(MIDS)] + far_bands[:half]
-    for s in range(2, steps):
-        for c in range(n):
-            acts.append(("rse", s, c))
-            acts += [("rs", s + 1, c)] if s + 1 < steps else [("div", c), ("agz", c)]
-    acts += far_bands[half:]
-    for name in ("agp", "agc", "age"):
-        acts += [(name, c) for c in range(n)]
-    return acts + [("finish",)]
-
-
-def fold_kernel(n_gx, n_gy, margin, chunks, acc, probe, sums, out_obj, out_probe, *scratch):
-    (from_near, from_far, vsend, vrecv, part, inbox, sems) = scratch
+def step_kernel(n_gx, n_gy, margin, offs, ext, probe, amp, table, out_obj, out_probe, *scratch):
+    (win, psi, xbuf, ybuf, ffwd, yback, fback, half, fr, frt, pads, acc, sums) = scratch[:13]
+    (from_near, from_far, vsend, vrecv, part, inbox, sems) = scratch[13:]
+    positions = amp.shape[0]
     gx, gy = lax.axis_index("gx"), lax.axis_index("gy")
     rows, cols = out_obj.shape[1], out_obj.shape[2]
     planes, extent = sums.shape[0], sums.shape[1]
@@ -306,6 +154,7 @@
     half_at = (mt + (1 - odd) * (ct - mt), mt + odd * (ct - mt))
     plan = reduce_plan(n_gx, n_gy)
     steps = len(plan)
+    chunks = [(0, 1)] + [(2 * i + 1, 2 * i + 3) for i in range(modes)]
 
     def swap(field, d, bits):
         out = 0
@@ -325,7 +174,10 @@
                     peers.append((px + nx * py, (gx + (px - fx) * (1 << bx), gy + (py - fy) * (1 << by))))
         return nx * ny, fx + nx * fy, peers
 
-    greet([up, down, near, far] + [dev for g in plan for _, dev in members(*g)[2]])
+    friends = [up, down, near, far] + [dev for g in plan for _, dev in members(*g)[2]]
+    barrier = pltpu.get_barrier_semaphore()
+    for device in friends:
+        pl.semaphore_signal(barrier, inc=1, device_id=device, device_id_type=MESH)
 
     slot = [0]
     pending = []
@@ -477,10 +329,221 @@
                     ends = jnp.concatenate([vrecv[1, side, c, t], vrecv[0, side, c, t]], 0)
                     out_obj[c, :, dst] = (base + ends) / scale
 
-    ops = {"rs": rs, "rse": rse, "div": div, "agz": agz, "agp": agp, "agc": agc, "age": age, "corner": corner, "mid": mid, "vert": vert, "power": power, "finish": finish}
-    for name, *args in fold_schedule(steps, len(chunks)):
-        ops[name](*args)
-    assert not flight, flight
+    starts = range(0, extent, CHUNK)
+
+    last = ext.shape[1] - extent // LANE - 1
+    c, s = table[:, :extent], table[:, extent:]
+    fr[:extent, :extent] = c
+    fr[:extent, extent:] = s
+    fr[extent:, :extent] = -s
+    fr[extent:, extent:] = c
+    frt[:extent, :extent] = c
+    frt[:extent, extent:] = -s
+    frt[extent:, :extent] = s
+    frt[extent:, extent:] = c
+
+    lane = lax.broadcasted_iota(jnp.int32, (CHUNK, LANE), 1)
+
+    def place(p):
+        c0 = offs[0, 1, p] + margin
+        tile = jnp.minimum(c0 // LANE, last)
+        return offs[0, 0, p] + margin, tile, c0 - tile * LANE
+
+    def add(plane, here, value, p):
+        if p == 0:
+            sums[plane, here, :] = value
+        else:
+            sums[plane, here, :] += value
+
+    def extract(p, rb):
+        r0, tile, low = place(p)
+        here = pl.ds(rb, CHUNK)
+        w = []
+        for c in range(2):
+            line = [
+                pltpu.roll(ext[c, tile + t, pl.ds(r0 + rb, CHUNK), :], lax.rem(LANE - low, LANE), 1)
+                for t in range(extent // LANE + 1)
+            ]
+            line = [jnp.where(lane < LANE - low, a, b) for a, b in zip(line, line[1:])]
+            w.append(jnp.concatenate(line, 1))
+            win[p, c, here, :] = w[c]
+        add(0, here, w[0] * w[0] + w[1] * w[1], p)
+        for k in range(modes):
+            cols = slice(k * extent, (k + 1) * extent)
+            pr, pi = probe[k, 0, here, :], probe[k, 1, here, :]
+            psi_re = pr * w[0] - pi * w[1]
+            psi_im = pr * w[1] + pi * w[0]
+            psi[p, k, 0, here, :] = psi_re
+            psi[p, k, 1, here, :] = psi_im
+            xbuf[p, here, cols] = psi_re.astype(BF16)
+            xbuf[p, pl.ds(extent + rb, CHUNK), cols] = psi_im.astype(BF16)
+
+    def rows_pass(p, c):
+        band = fr[c * extent : (c + 1) * extent, :]
+        out = jnp.dot(band, xbuf[p], preferred_element_type=F32).astype(BF16)
+        for k in range(modes):
+            ybuf[k * extent : (k + 1) * extent, c * extent : (c + 1) * extent] = out[
+                :, k * extent : (k + 1) * extent
+            ]
+
+    def cols_pass(p, k):
+        band = slice(k * extent, (k + 1) * extent)
+        ffwd[p % 2, band, :] = jnp.dot(ybuf[band, :], frt[...], preferred_element_type=F32)
+
+    def rows_back(k, p, c):
+        band = frt[c * extent : (c + 1) * extent, :]
+        cols = slice(k * extent, (k + 1) * extent)
+        out = jnp.dot(band, xbuf[p, :, cols], preferred_element_type=F32)
+        yback[p % 2, :, c * extent : (c + 1) * extent] = out.astype(BF16)
+
+    def cols_back(k, p):
+        fback[p % 2] = jnp.dot(yback[p % 2], fr[...], preferred_element_type=F32)
+
+    def project(p, rb):
+        q = p % 2
+        parts = []
+        intensity = jnp.zeros((CHUNK, extent), F32)
+        for k in range(modes):
+            at = pl.ds(k * extent + rb, CHUNK)
+            re, im = ffwd[q, at, :extent], ffwd[q, at, extent:]
+            intensity += re * re + im * im
+            parts.append((re, im))
+        factor = amp[p, pl.ds(rb, CHUNK), :] * jnp.minimum(lax.rsqrt(intensity), 4.0)
+        for k in range(modes):
+            cols = slice(k * extent, (k + 1) * extent)
+            xbuf[p, pl.ds(rb, CHUNK), cols] = (parts[k][0] * factor).astype(BF16)
+            xbuf[p, pl.ds(extent + rb, CHUNK), cols] = (parts[k][1] * factor).astype(BF16)
+
+    def correct(k, p, rb):
+        here = pl.ds(rb, CHUNK)
+        wr, wi = win[p, 0, here, :], win[p, 1, here, :]
+        dr = fback[p % 2, here, :extent] - psi[p, k, 0, here, :]
+        di = fback[p % 2, here, extent:] - psi[p, k, 1, here, :]
+        pr, pi = probe[k, 0, here, :], probe[k, 1, here, :]
+        add(2 * k + 1, here, wr * dr + wi * di, p)
+        add(2 * k + 2, here, wr * di - wi * dr, p)
+        value = [pr * dr + pi * di, pr * di - pi * dr]
+        if k:
+            value = [half[p, c, here, :] + value[c] for c in range(2)]
+        if k + 1 < modes:
+            for c in range(2):
+                half[p, c, here, :] = value[c]
+            return
+        _, _, low = place(p)
+        blank = jnp.zeros((CHUNK, LANE), F32)
+        for c in range(2):
+            line = [
+                pltpu.roll(value[c][:, t * LANE : (t + 1) * LANE], lax.rem(low, LANE), 1)
+                for t in range(extent // LANE)
+            ]
+            for t, (a, b) in enumerate(zip([blank] + line, line + [blank])):
+                pads[p, c, t, pl.ds(CHUNK + rb, CHUNK), :] = jnp.where(lane < low, a, b)
+
+    def blank_pads(p):
+        for at in (0, CHUNK + extent):
+            pads[p, :, :, at : at + CHUNK, :] = jnp.zeros((2, pads.shape[2], CHUNK, LANE), F32)
+
+    def gather(lo, hi):
+        tiles = pads.shape[2]
+        for at in range(lo, hi, CHUNK):
+            for t in range(acc.shape[1]):
+                spots = []
+                for p in range(positions):
+                    r0, tile, _ = place(p)
+                    row = jnp.clip(at - r0, -CHUNK, extent) + CHUNK
+                    inside = (t >= tile) & (t < tile + tiles)
+                    spots.append((p, jnp.clip(t - tile, 0, tiles - 1), jnp.where(inside, row, 0)))
+                for c in range(2):
+                    total = None
+                    for p, tile, row in spots:
+                        value = pads[p, c, tile, pl.ds(row, CHUNK), :]
+                        total = value if total is None else total + value
+                    acc[c, t, at : at + CHUNK, :] = total
+
+    def beside(matmuls, others):
+        n = len(matmuls)
+        for i, (call, args) in enumerate(matmuls):
+            call(*args)
+            for other, rest in others[i * len(others) // n : (i + 1) * len(others) // n]:
+                other(*rest)
+
+    for rb in starts:
+        extract(0, rb)
+    for p in range(positions):
+        beside(
+            [(rows_pass, (p, 0)), (rows_pass, (p, 1))] + [(cols_pass, (p, k)) for k in range(modes)],
+            [(blank_pads, (p,))]
+            + ([(project, (p - 1, rb)) for rb in starts] if p else [])
+            + ([(extract, (p + 1, rb)) for rb in starts] if p + 1 < positions else []),
+        )
+    for rb in starts:
+        project(positions - 1, rb)
+    pl.semaphore_wait(barrier, len(friends))
+    rs(0, 0)
+
+    def back(k, p):
+        return [(rows_back, (k, p, 0)), (rows_back, (k, p, 1)), (cols_back, (k, p))]
+
+    units = [(k, p) for k in range(modes) for p in range(positions)]
+    beside(back(*units[0]), [])
+    for u, (k, p) in enumerate(units):
+        rest = [(correct, (k, p, rb)) for rb in starts]
+        if u + 1 < len(units):
+            beside(back(*units[u + 1]), rest)
+        else:
+            for call, args in rest:
+                call(*args)
+        if u == 2:
+            rse(0, 0)
+            rs(1, 0)
+        if p + 1 == positions:
+            rs(0, 1 + k)
+
+    bands = [(b, i) for i in range(PIECES) for b in (0, 1)]
+
+    def corners(side):
+        for b, i in bands:
+            corner(side, b, i)
+
+    n = len(chunks)
+    for c in range(1, n - 1):
+        rse(0, c)
+        rs(1, c)
+    gather(0, m)
+    gather(m + rows, m + rows + m)
+    corners(0)
+    rse(1, 0)
+    rs(2, 0)
+    rse(0, n - 1)
+    rs(1, n - 1)
+    corners(1)
+    gather(m, m + rows)
+    power()
+    for b, i in bands:
+        vert(0, b, i)
+    for c in range(1, n):
+        rse(1, c)
+        rs(2, c)
+    for side in (1, 0):
+        for i in range(MIDS):
+            mid(side, i, MIDS)
+    for b, i in bands[: len(bands) // 2]:
+        vert(1, b, i)
+    for s in range(2, steps):
+        for c in range(n):
+            rse(s, c)
+            if s + 1 < steps:
+                rs(s + 1, c)
+            elif c:
+                div(c)
+                agz(c)
+    for b, i in bands[len(bands) // 2 :]:
+        vert(1, b, i)
+    for act in (agp, agc, age):
+        for c in range(1, n):
+            act(c)
+    finish()
+    assert not flight
     for copy in pending:
         copy.wait_send()
 
@@ -490,6 +553,7 @@
     modes = probe_field.shape[0]
     margin = extent // 2
     rows, cols = object_field.shape[1:]
+    positions = amplitude.shape[0]
     mt, ct = margin // LANE, cols // LANE
     ext_shape = (2, 2 * mt + ct, rows + 2 * margin, LANE)
     ext = pl.pallas_call(
@@ -503,58 +567,43 @@
     )(object_field)
 
     planes = 2 * modes + 1
-    acc, sums = pl.pallas_call(
-        functools.partial(update_kernel, margin),
-        out_shape=(
-            jax.ShapeDtypeStruct(ext_shape, F32),
-            jax.ShapeDtypeStruct((planes, extent, extent), F32),
-        ),
-        in_specs=[
-            pl.BlockSpec(memory_space=pltpu.SMEM),
-            VMEM,
-            VMEM,
-            VMEM,
-            VMEM,
-        ],
-        out_specs=(VMEM, VMEM),
-        scratch_shapes=[
-            pltpu.VMEM((2, 2, extent, extent), F32),
-            pltpu.VMEM((2, modes, 2, extent, extent), F32),
-            pltpu.VMEM((2, 2 * extent, modes * extent), BF16),
-            pltpu.VMEM((modes * extent, 2 * extent), BF16),
-            pltpu.VMEM((2, modes * extent, 2 * extent), F32),
-            pltpu.VMEM((2 * extent, 2 * extent), BF16),
-            pltpu.VMEM((2 * extent, 2 * extent), BF16),
-        ],
-        compiler_params=pltpu.CompilerParams(vmem_limit_bytes=LIMIT),
-        name="update",
-    )(offsets.transpose(1, 2, 0), ext, probe_field, amplitude[:, 0], dft_tables(extent))
-
     plan = reduce_plan(n_gx, n_gy)
     peers = sum((1 << (cx + cy)) - 1 for _, cx, _, cy in plan)
-    chunks = ((0, modes + 1), (modes + 1, planes))
     out_obj, out_probe = pl.pallas_call(
-        functools.partial(fold_kernel, n_gx, n_gy, margin, chunks),
+        functools.partial(step_kernel, n_gx, n_gy, margin),
         out_shape=(
             jax.ShapeDtypeStruct(object_field.shape, F32),
             jax.ShapeDtypeStruct((2 * modes, extent, extent), F32),
         ),
-        in_specs=[VMEM] * 3,
+        in_specs=[pl.BlockSpec(memory_space=pltpu.SMEM), VMEM, VMEM, VMEM, VMEM],
         out_specs=(VMEM, VMEM),
         scratch_shapes=[
+            pltpu.VMEM((positions, 2, extent, extent), F32),
+            pltpu.VMEM((positions, modes, 2, extent, extent), F32),
+            pltpu.VMEM((positions, 2 * extent, modes * extent), BF16),
+            pltpu.VMEM((modes * extent, 2 * extent), BF16),
+            pltpu.VMEM((2, modes * extent, 2 * extent), F32),
+            pltpu.VMEM((2, extent, 2 * extent), BF16),
+            pltpu.VMEM((2, extent, 2 * extent), F32),
+            pltpu.VMEM((positions, 2, extent, extent), F32),
+            pltpu.VMEM((2 * extent, 2 * extent), BF16),
+            pltpu.VMEM((2 * extent, 2 * extent), BF16),
+            pltpu.VMEM((positions, 2, extent // LANE + 1, extent + 2 * CHUNK, LANE), F32),
+            pltpu.VMEM(ext_shape, F32),
+            pltpu.VMEM((planes, extent, extent), F32),
             pltpu.VMEM((2, mt, rows + 2 * margin, LANE), F32),
             pltpu.VMEM((2, mt, rows + 2 * margin, LANE), F32),
             pltpu.VMEM((2, 2, 2, mt, margin, LANE), F32),
             pltpu.VMEM((2, 2, 2, mt, margin, LANE), F32),
             pltpu.VMEM((len(plan), planes, extent, extent), F32),
-            pltpu.VMEM((planes, 3 * extent, extent), F32),
-            pltpu.SemaphoreType.DMA((2, 8 * PIECES + 2 * MIDS + (peers + 24) * len(chunks))),
+            pltpu.VMEM((planes, 2 * extent, extent), F32),
+            pltpu.SemaphoreType.DMA((2, 8 * PIECES + 2 * MIDS + (peers + 24) * (modes + 1))),
         ],
         compiler_params=pltpu.CompilerParams(
-            collective_id=1, has_side_effects=True, vmem_limit_bytes=LIMIT
+            collective_id=1, has_side_effects=True, vmem_limit_bytes=STEP_LIMIT
         ),
-        name="fold",
-    )(acc, probe_field, sums)
+        name="step",
+    )(offsets.transpose(1, 2, 0), ext, probe_field, amplitude[:, 0], dft_tables(extent))
     return object_field + out_obj, probe_field + out_probe.reshape(probe_field.shape)
 
 

time: 65.3 us -> 60.9 us (0.933)
  Pallas kernels: 61.3 us -> 56.8 us
    pallas_call x2 -> x1, Pallas kernels: 42.8 us -> 38.4 us  [body(): pl.pallas_call(functools.partial(step_kernel, n_gx, n_gy, margin), out_sh...]
where the time goes in v4:
time: 60.9 us; the launch traced here: 60.6 us
  Pallas kernels  56.8 us (93%)
  other arithmetic  1.97 us (3%)
  local copies, waits for them, and re-layouts  1.15 us (2%)
  between operations  0.71 us (1%)
    pallas_call x1, Pallas kernels, body(): pl.pallas_call(functools.partial(step_kernel, n_gx, n_gy, margin), out_sh...  38.4 us
    pallas_call x1, Pallas kernels, body(): pl.pallas_call(functools.partial(halo_kernel, n_gx, n_gy, margin), out_sh...  18.4 us

profile of v4, /device:TPU:0, one launch (start us, length us, event | category | flops | bytes accessed | tf_op | source)
XLA Modules:
  0.0 60.6 jit_solution(13176683925187071084)
XLA Ops:
  0.6 0.0 copy-start
  0.6 0.0 copy-start.1
  0.7 1.1 %copy-done.1 = f32[2,256,256]{2,1,0:T(8,128)S(1)} copy-done((f32[2,256,256]{2,1,0:T(8,128)S(1)}, f32[2,256,256]{2,1,0:T(8,128)}, u32[]{:S(2)}) %copy-start.1) | copy-done | bytes 524312
  1.8 0.0 copy-start.3
  1.8 0.0 copy-start.4
  1.8 0.0 copy-start.5
  1.8 18.4 %halo.1.ext = f32[2,4,512,128]{3,2,1,0:T(8,128)S(1)} custom-call(f32[2,256,256]{2,1,0:T(8,128)S(1)} %copy-done.1), custom_call_target="tpu_custom_call" | custom-call | tf_op jit(solution)/shard_map/halo/pallas_call | solution.py:559
  20.2 0.0 copy-done
  20.2 0.0 copy-done.3
  20.2 0.0 copy-done.4
  20.2 0.0 copy-done.5
  20.2 0.0 copy-start.2
  20.3 38.4 %step.1 = (f32[2,256,256]{2,1,0:T(8,128)S(1)}, f32[4,256,256]{2,1,0:T(8,128)S(1)}) custom-call(s32[1,2,4]{2,1,0:T(2,128)S(1)} %bitcast.5, f32[2,4,512,128]{3,2,1,0:T(8,128)S(1)} %halo.1.ext, f32[2,2,256,256]{3,2,1,0:T(8,128)S(1)} %copy-done, f32[4,256,256]{2,1,0:T(8,128)S(1)} %bitcast.3, bf16[256,512]{1,0:T(8,128)(2,1)S(1)} %copy-done.4), custom_call_target="tpu_custom_call" | custom-call | tf_op jit(solution)/shard_map/step/pallas_call | solution.py:572
  58.7 0.0 copy-done.2
  58.7 0.9 %add.6 = f32[2,256,256]{2,1,0:T(8,128)} add(f32[2,256,256]{2,1,0:T(8,128)S(1)} %copy-done.2, f32[2,256,256]{2,1,0:T(8,128)S(1)} %get-tuple-element.4) | non-fusion elementwise | flops 131072 | bytes 1572864 | tf_op jit(solution)/shard_map/add | solution.py:607
  59.5 1.1 %add.7 = f32[2,2,256,256]{3,2,1,0:T(8,128)} add(f32[2,2,256,256]{3,2,1,0:T(8,128)S(1)} %copy-done, f32[2,2,256,256]{3,2,1,0:T(8,128)S(1)} %bitcast.4) | non-fusion elementwise | flops 262144 | bytes 3145728 | tf_op jit(solution)/shard_map/add | solution.py:607
Async XLA Ops:
  0.6 19.6 %copy-start = (f32[2,2,256,256]{3,2,1,0:T(8,128)S(1)}, f32[2,2,256,256]{3,2,1,0:T(8,128)}, u32[]{:S(2)}) copy-start(f32[2,2,256,256]{3,2,1,0:T(8,128)} %probe.1) | copy-start | bytes 3145732
  0.6 1.1 %copy-start.1 = (f32[2,256,256]{2,1,0:T(8,128)S(1)}, f32[2,256,256]{2,1,0:T(8,128)}, u32[]{:S(2)}) copy-start(f32[2,256,256]{2,1,0:T(8,128)} %obj.1) | copy-start | bytes 1572868
  1.8 18.4 %copy-start.3 = (f32[4,1,256,256]{3,2,1,0:T(8,128)S(1)}, f32[4,1,256,256]{3,2,1,0:T(8,128)}, u32[]{:S(2)}) copy-start(f32[4,1,256,256]{3,2,1,0:T(8,128)} %param.7) | copy-start | bytes 3145732
  1.8 18.5 %copy-start.4 = (bf16[256,512]{1,0:T(8,128)(2,1)S(1)}, bf16[256,512]{1,0:T(8,128)(2,1)}, u32[]{:S(2)}) copy-start(bf16[256,512]{1,0:T(8,128)(2,1)} %constant.2.clone.table) | copy-start | bytes 786436
  1.8 18.5 %copy-start.5 = (s32[4,1,2]{0,2,1:T(2,128)S(1)}, s32[4,1,2]{0,2,1:T(2,128)}, u32[]{:S(2)}) copy-start(s32[4,1,2]{0,2,1:T(2,128)} %param.8) | copy-start | bytes 100
  20.2 38.4 %copy-start.2 = (f32[2,256,256]{2,1,0:T(8,128)S(1)}, f32[2,256,256]{2,1,0:T(8,128)}, u32[]{:S(2)}) copy-start(f32[2,256,256]{2,1,0:T(8,128)} %obj.1) | copy-start | bytes 1572868

commit v5 on v4

--- a/solution.py
+++ b/solution.py
@@ -121,10 +121,13 @@
         own.wait()
 
 
-def reduce_plan(n_gx, n_gy):
+def reduce_plan(n_gx, n_gy, kind):
     x_bits, y_bits = n_gx.bit_length() - 1, n_gy.bit_length() - 1
-    steps = [(0, 0, 0, 1), (0, 1, 1, 1)]
-    steps.append((1, min(2, x_bits - 1), 0, 0))
+    steps = [(0, 0, 0, 1)]
+    if kind == "x":
+        steps += [(0, 1, 0, 0), (1, min(2, x_bits - 1), 1, 1)]
+    else:
+        steps += [(0, 0, 1, 1), (0, min(3, x_bits), 0, 0)]
     for b in range(3, x_bits, 2):
         steps.append((b, min(2, x_bits - b), 0, 0))
     for b in range(2, y_bits, 2):
@@ -132,7 +135,13 @@
     return steps
 
 
-def step_kernel(n_gx, n_gy, margin, offs, ext, probe, amp, table, out_obj, out_probe, *scratch):
+def reduce_chunks(modes):
+    planes = 2 * modes + 1
+    chunks = [(0, 1, "x", 0), (0, 1, "y", planes)]
+    return chunks + [(2 * k + 1, 2 * k + 3, "xy"[k % 2], 2 * k + 1) for k in range(modes)]
+
+
+def step_kernel(n_gx, n_gy, margin, offs, ext, obj, probe, amp, table, out_obj, out_probe, *scratch):
     (win, psi, xbuf, ybuf, ffwd, yback, fback, half, fr, frt, pads, acc, sums) = scratch[:13]
     (from_near, from_far, vsend, vrecv, part, inbox, sems) = scratch[13:]
     positions = amp.shape[0]
@@ -152,9 +161,9 @@
     came = (from_near, from_far)
     halo_at = ((1 - odd) * (mt + ct), odd * (mt + ct))
     half_at = (mt + (1 - odd) * (ct - mt), mt + odd * (ct - mt))
-    plan = reduce_plan(n_gx, n_gy)
-    steps = len(plan)
-    chunks = [(0, 1)] + [(2 * i + 1, 2 * i + 3) for i in range(modes)]
+    plans = {kind: reduce_plan(n_gx, n_gy, kind) for kind in "xy"}
+    steps = len(plans["x"])
+    chunks = reduce_chunks(modes)
 
     def swap(field, d, bits):
         out = 0
@@ -174,7 +183,9 @@
                     peers.append((px + nx * py, (gx + (px - fx) * (1 << bx), gy + (py - fy) * (1 << by))))
         return nx * ny, fx + nx * fy, peers
 
-    friends = [up, down, near, far] + [dev for g in plan for _, dev in members(*g)[2]]
+    friends = [up, down, near, far] + [
+        dev for plan in plans.values() for g in plan for _, dev in members(*g)[2]
+    ]
     barrier = pltpu.get_barrier_semaphore()
     for device in friends:
         pl.semaphore_signal(barrier, inc=1, device_id=device, device_id_type=MESH)
@@ -189,56 +200,66 @@
         pending.append(copy)
         return copy
 
-    state = [{"off": 0, "n": extent, "src": sums, "box": 0} for _ in chunks]
+    state = [{"off": 0, "n": extent, "src": (sums, lo, hi), "box": 0} for lo, hi, _, _ in chunks]
     history = [[] for _ in chunks]
     flight = {}
 
     def rws(at, n):
         return pl.ds(pl.multiple_of(at, SUB), n)
 
+    def slots(c):
+        lo, hi, _, slot = chunks[c]
+        return slice(slot, slot + hi - lo)
+
     def rs(step, c):
-        lo, hi = chunks[c]
         s = state[c]
-        size, mine, peers = members(*plan[step])
+        size, mine, peers = members(*plans[chunks[c][2]][step])
         split = step < 3
         n = s["n"] // size if split else s["n"]
+        src, lo, hi = s["src"]
         copies = []
         for field, device in peers:
             give = s["off"] + field * n if split else s["off"]
-            box = s["box"] + mine * n
-            copies.append(send(s["src"].at[lo:hi, rws(give, n), :], inbox.at[lo:hi, rws(box, n), :], device))
+            box = inbox.at[slots(c), rws(s["box"] + mine * n, n), :]
+            copies.append(send(src.at[lo:hi, rws(give, n), :], box, device))
         keep = s["off"] + mine * n if split else s["off"]
         history[c].append((size, mine, peers, split))
         flight["rs", step, c] = (copies, keep, n, size, mine, [f for f, _ in peers], s["box"], split)
         s["box"] += size * n
 
     def rse(step, c):
-        lo, hi = chunks[c]
+        at = slots(c)
         copies, keep, n, size, mine, fields, box, split = flight.pop(("rs", step, c))
         s = state[c]
         for copy in copies:
             copy.wait_recv()
-        own = s["src"][lo:hi, rws(keep, n), :]
+        src, lo, hi = s["src"]
+        own = src[lo:hi, rws(keep, n), :]
         if split:
             total = own
             for f in fields:
-                total += inbox[lo:hi, rws(box + f * n, n), :]
+                total += inbox[at, rws(box + f * n, n), :]
         else:
-            inbox[lo:hi, rws(box + mine * n, n), :] = own
-            total = inbox[lo:hi, rws(box, n), :]
+            inbox[at, rws(box + mine * n, n), :] = own
+            total = inbox[at, rws(box, n), :]
             for j in range(1, size):
-                total += inbox[lo:hi, rws(box + j * n, n), :]
-        part[step, lo:hi, rws(keep, n), :] = total
-        s["off"], s["n"], s["src"] = keep, n, part.at[step]
+                total += inbox[at, rws(box + j * n, n), :]
+        part[step, at, rws(keep, n), :] = total
+        s["off"], s["n"], s["src"] = keep, n, (part.at[step], at.start, at.stop)
+
+    def follow(c, other):
+        state[c] = dict(state[other], box=0)
+        history[c] = list(history[other])
 
     def div(c):
-        lo, hi = chunks[c]
-        first = 1 if lo == 0 else 0
+        lo, hi, kind, slot = chunks[c]
         s = state[c]
         keep = rws(s["off"], s["n"])
-        weight = s["src"][0, keep, :] + 1e-05
-        for k in range(lo + first, hi):
-            out_probe[k - 1, keep, :] = s["src"][k, keep, :] / weight
+        weight = part[steps - 1, slots("xy".index(kind)).start, keep, :] + 1e-05
+        for k in range(lo, hi):
+            mode, c = divmod(k - 1, 2)
+            step = part[steps - 1, slot + k - lo, keep, :] / weight
+            out_probe[k - 1, keep, :] = probe[mode, c, keep, :] + step
 
     def planes_of(c):
         lo, hi = chunks[c][:2]
@@ -327,7 +348,7 @@
                 for c in range(2):
                     base = acc[c, half_at[side] + t, pl.ds(m, rows), :] + came[side][c, t, pl.ds(m, rows), :]
                     ends = jnp.concatenate([vrecv[1, side, c, t], vrecv[0, side, c, t]], 0)
-                    out_obj[c, :, dst] = (base + ends) / scale
+                    out_obj[c, :, dst] = obj[c, :, dst] + (base + ends) / scale
 
     starts = range(0, extent, CHUNK)
 
@@ -495,54 +516,60 @@
                 call(*args)
         if u == 2:
             rse(0, 0)
+            follow(1, 0)
             rs(1, 0)
+            rs(1, 1)
         if p + 1 == positions:
-            rs(0, 1 + k)
+            rs(0, 2 + k)
 
     bands = [(b, i) for i in range(PIECES) for b in (0, 1)]
-
-    def corners(side):
-        for b, i in bands:
-            corner(side, b, i)
-
-    n = len(chunks)
-    for c in range(1, n - 1):
+    half_way = len(bands) // 2
+    early, late = range(2, len(chunks) - 1), len(chunks) - 1
+
+    for c in early:
         rse(0, c)
         rs(1, c)
     gather(0, m)
     gather(m + rows, m + rows + m)
-    corners(0)
-    rse(1, 0)
-    rs(2, 0)
-    rse(0, n - 1)
-    rs(1, n - 1)
-    corners(1)
+    for b, i in bands:
+        corner(0, b, i)
+    for c in (0, 1):
+        rse(1, c)
+        rs(2, c)
+    rse(0, late)
+    rs(1, late)
+    for b, i in bands:
+        corner(1, b, i)
     gather(m, m + rows)
     power()
-    for b, i in bands:
+    for b, i in bands[:half_way]:
         vert(0, b, i)
-    for c in range(1, n):
+    for c in range(2, len(chunks)):
         rse(1, c)
         rs(2, c)
+    for b, i in bands[half_way:]:
+        vert(0, b, i)
     for side in (1, 0):
         for i in range(MIDS):
             mid(side, i, MIDS)
-    for b, i in bands[: len(bands) // 2]:
+    for b, i in bands[:half_way]:
         vert(1, b, i)
     for s in range(2, steps):
-        for c in range(n):
+        for c in range(len(chunks)):
             rse(s, c)
             if s + 1 < steps:
                 rs(s + 1, c)
-            elif c:
+            elif c >= 2:
                 div(c)
                 agz(c)
-    for b, i in bands[len(bands) // 2 :]:
+    for b, i in bands[half_way:]:
         vert(1, b, i)
-    for act in (agp, agc, age):
-        for c in range(1, n):
+    for act in (agp, agc):
+        for c in range(2, len(chunks)):
             act(c)
     finish()
+    for c in range(2, len(chunks)):
+        age(c)
     assert not flight
     for copy in pending:
         copy.wait_send()
@@ -567,15 +594,17 @@
     )(object_field)
 
     planes = 2 * modes + 1
-    plan = reduce_plan(n_gx, n_gy)
-    peers = sum((1 << (cx + cy)) - 1 for _, cx, _, cy in plan)
+    steps = len(reduce_plan(n_gx, n_gy, "x"))
+    peers = max(
+        sum((1 << (cx + cy)) - 1 for _, cx, _, cy in reduce_plan(n_gx, n_gy, kind)) for kind in "xy"
+    )
     out_obj, out_probe = pl.pallas_call(
         functools.partial(step_kernel, n_gx, n_gy, margin),
         out_shape=(
             jax.ShapeDtypeStruct(object_field.shape, F32),
             jax.ShapeDtypeStruct((2 * modes, extent, extent), F32),
         ),
-        in_specs=[pl.BlockSpec(memory_space=pltpu.SMEM), VMEM, VMEM, VMEM, VMEM],
+        in_specs=[pl.BlockSpec(memory_space=pltpu.SMEM)] + [VMEM] * 5,
         out_specs=(VMEM, VMEM),
         scratch_shapes=[
             pltpu.VMEM((positions, 2, extent, extent), F32),
@@ -595,16 +624,16 @@
             pltpu.VMEM((2, mt, rows + 2 * margin, LANE), F32),
             pltpu.VMEM((2, 2, 2, mt, margin, LANE), F32),
             pltpu.VMEM((2, 2, 2, mt, margin, LANE), F32),
-            pltpu.VMEM((len(plan), planes, extent, extent), F32),
-            pltpu.VMEM((planes, 2 * extent, extent), F32),
-            pltpu.SemaphoreType.DMA((2, 8 * PIECES + 2 * MIDS + (peers + 24) * (modes + 1))),
+            pltpu.VMEM((steps, planes + 1, extent, extent), F32),
+            pltpu.VMEM((planes + 1, 2 * extent, extent), F32),
+            pltpu.SemaphoreType.DMA((2, 8 * PIECES + 2 * MIDS + (peers + 24) * (modes + 2))),
         ],
         compiler_params=pltpu.CompilerParams(
             collective_id=1, has_side_effects=True, vmem_limit_bytes=STEP_LIMIT
         ),
         name="step",
-    )(offsets.transpose(1, 2, 0), ext, probe_field, amplitude[:, 0], dft_tables(extent))
-    return object_field + out_obj, probe_field + out_probe.reshape(probe_field.shape)
+    )(offsets.transpose(1, 2, 0), ext, object_field, probe_field, amplitude[:, 0], dft_tables(extent))
+    return out_obj, out_probe.reshape(probe_field.shape)
 
 
 def solution(mesh):

time: 60.9 us -> 64.1 us (1.053)
  Pallas kernels: 56.8 us -> 59.5 us
  local copies, waits for them, and re-layouts: 1.15 us -> 3.77 us
  other arithmetic: 1.97 us -> 0 us
    pallas_call x1, Pallas kernels: 38.4 us -> 41.1 us  [body(): pl.pallas_call(functools.partial(step_kernel, n_gx, n_gy, margin), out_sh...]
    unnamed x12 -> x14, local copies, waits for them, and re-layouts: 1.15 us -> 3.77 us
    add x2 -> x0, other arithmetic: 1.97 us -> none  [the longest x1 1.1 us: body(): probe_field + out_probe.reshape(probe_field.shape)]
where the time goes in v5:
time: 64.1 us; the launch traced here: 64 us
  Pallas kernels  59.5 us (93%)
  local copies, waits for them, and re-layouts  3.77 us (6%)
  between operations  0.7 us (1%)
    pallas_call x1, Pallas kernels, body(): pl.pallas_call(functools.partial(step_kernel, n_gx, n_gy, margin), out_sh...  41.1 us
    pallas_call x1, Pallas kernels, body(): pl.pallas_call(functools.partial(halo_kernel, n_gx, n_gy, margin), out_sh...  18.4 us
    unnamed x14, local copies, waits for them, and re-layouts  3.77 us

profile of v5, /device:TPU:0, one launch (start us, length us, event | category | flops | bytes accessed | tf_op | source)
XLA Modules:
  0.0 64.0 jit_solution(16267508117890597557)
XLA Ops:
  0.6 0.0 copy-start.5
  0.6 0.0 copy-start
  0.7 1.0 %copy-done = f32[2,256,256]{2,1,0:T(8,128)S(1)} copy-done((f32[2,256,256]{2,1,0:T(8,128)S(1)}, f32[2,256,256]{2,1,0:T(8,128)}, u32[]{:S(2)}) %copy-start) | copy-done | bytes 524312
  1.7 0.0 copy-start.1
  1.7 0.0 copy-start.2
  1.7 0.0 copy-start.3
  1.7 18.4 %halo.1.ext = f32[2,4,512,128]{3,2,1,0:T(8,128)S(1)} custom-call(f32[2,256,256]{2,1,0:T(8,128)S(1)} %copy-done), custom_call_target="tpu_custom_call" | custom-call | tf_op jit(solution)/shard_map/halo/pallas_call | solution.py:586
  20.1 0.0 copy-done.5
  20.1 0.0 copy-done.1
  20.1 0.0 copy-done.2
  20.2 0.0 copy-done.3
  20.2 0.0 copy-start.4
  20.2 0.9 %copy-done.4 = bf16[256,512]{1,0:T(8,128)(2,1)S(1)} copy-done((bf16[256,512]{1,0:T(8,128)(2,1)S(1)}, bf16[256,512]{1,0:T(8,128)(2,1)}, u32[]{:S(2)}) %copy-start.4) | copy-done | bytes 262168
  21.1 41.1 %step.1 = (f32[2,256,256]{2,1,0:T(8,128)S(1)}, f32[4,256,256]{2,1,0:T(8,128)S(1)}) custom-call(s32[1,2,4]{2,1,0:T(2,128)S(1)} %bitcast.5, f32[2,4,512,128]{3,2,1,0:T(8,128)S(1)} %halo.1.ext, f32[2,256,256]{2,1,0:T(8,128)S(1)} %copy-done.1, f32[2,2,256,256]{3,2,1,0:T(8,128)S(1)} %copy-done.2, f32[4,256,256]{2,1,0:T(8,128)S(1)} %bitcast.4, ...), custom_call_target="tpu_custom_call" | custom-call | tf_op jit(solution)/shard_map/step/pallas_call | solution.py:601
  62.2 0.8 %copy.9 = f32[2,256,256]{2,1,0:T(8,128)} copy(f32[2,256,256]{2,1,0:T(8,128)S(1)} %get-tuple-element.8) | data formatting | bytes 1048576
  63.0 1.0 %copy.10 = f32[2,2,256,256]{3,2,1,0:T(8,128)} copy(f32[2,2,256,256]{3,2,1,0:T(8,128)S(1)} %bitcast.3) | data formatting | bytes 2097152
Async XLA Ops:
  0.6 19.5 %copy-start.5 = (s32[4,1,2]{0,2,1:T(2,128)S(1)}, s32[4,1,2]{0,2,1:T(2,128)}, u32[]{:S(2)}) copy-start(s32[4,1,2]{0,2,1:T(2,128)} %param.8) | copy-start | bytes 100
  0.6 1.0 %copy-start = (f32[2,256,256]{2,1,0:T(8,128)S(1)}, f32[2,256,256]{2,1,0:T(8,128)}, u32[]{:S(2)}) copy-start(f32[2,256,256]{2,1,0:T(8,128)} %obj.3) | copy-start | bytes 1572868
  1.7 18.4 %copy-start.1 = (f32[2,256,256]{2,1,0:T(8,128)S(1)}, f32[2,256,256]{2,1,0:T(8,128)}, u32[]{:S(2)}) copy-start(f32[2,256,256]{2,1,0:T(8,128)} %obj.3) | copy-start | bytes 1572868
  1.7 18.5 %copy-start.2 = (f32[2,2,256,256]{3,2,1,0:T(8,128)S(1)}, f32[2,2,256,256]{3,2,1,0:T(8,128)}, u32[]{:S(2)}) copy-start(f32[2,2,256,256]{3,2,1,0:T(8,128)} %probe.1) | copy-start | bytes 3145732
  1.7 18.5 %copy-start.3 = (f32[4,1,256,256]{3,2,1,0:T(8,128)S(1)}, f32[4,1,256,256]{3,2,1,0:T(8,128)}, u32[]{:S(2)}) copy-start(f32[4,1,256,256]{3,2,1,0:T(8,128)} %param.7) | copy-start | bytes 3145732
  20.2 1.0 %copy-start.4 = (bf16[256,512]{1,0:T(8,128)(2,1)S(1)}, bf16[256,512]{1,0:T(8,128)(2,1)}, u32[]{:S(2)}) copy-start(bf16[256,512]{1,0:T(8,128)(2,1)} %constant.2.clone.table) | copy-start | bytes 786436

commit v6 on v4

--- a/solution.py
+++ b/solution.py
@@ -484,6 +484,7 @@
     def back(k, p):
         return [(rows_back, (k, p, 0)), (rows_back, (k, p, 1)), (cols_back, (k, p))]
 
+    n = len(chunks)
     units = [(k, p) for k in range(modes) for p in range(positions)]
     beside(back(*units[0]), [])
     for u, (k, p) in enumerate(units):
@@ -493,6 +494,10 @@
         else:
             for call, args in rest:
                 call(*args)
+        if u + 2 == len(units):
+            for c in range(1, n - 1):
+                rse(0, c)
+                rs(1, c)
         if u == 2:
             rse(0, 0)
             rs(1, 0)
@@ -505,10 +510,6 @@
         for b, i in bands:
             corner(side, b, i)
 
-    n = len(chunks)
-    for c in range(1, n - 1):
-        rse(0, c)
-        rs(1, c)
     gather(0, m)
     gather(m + rows, m + rows + m)
     corners(0)
@@ -527,7 +528,7 @@
     for side in (1, 0):
         for i in range(MIDS):
             mid(side, i, MIDS)
-    for b, i in bands[: len(bands) // 2]:
+    for b, i in bands:
         vert(1, b, i)
     for s in range(2, steps):
         for c in range(n):
@@ -537,12 +538,12 @@
             elif c:
                 div(c)
                 agz(c)
-    for b, i in bands[len(bands) // 2 :]:
-        vert(1, b, i)
-    for act in (agp, agc, age):
+    for act in (agp, agc):
         for c in range(1, n):
             act(c)
     finish()
+    for c in range(1, n):
+        age(c)
     assert not flight
     for copy in pending:
         copy.wait_send()
@@ -564,7 +565,7 @@
         scratch_shapes=[pltpu.SemaphoreType.DMA((2, (2 + 8 * STRIPS) * mt)), pltpu.SemaphoreType.DMA((ct,))],
         compiler_params=pltpu.CompilerParams(collective_id=0, has_side_effects=True, vmem_limit_bytes=LIMIT),
         name="halo",
-    )(object_field)
+    )(pltpu.with_memory_space_constraint(object_field, pltpu.MemorySpace.HBM))
 
     planes = 2 * modes + 1
     plan = reduce_plan(n_gx, n_gy)

time: 60.9 us -> 59.5 us (0.977)
  local copies, waits for them, and re-layouts: 1.15 us -> 0.03 us
    unnamed x12 -> x10, local copies, waits for them, and re-layouts: 1.15 us -> 0.03 us
where the time goes in v6:
time: 59.5 us; the launch traced here: 59.4 us
  Pallas kernels  56.7 us (95%)
  other arithmetic  1.97 us (3%)
  between operations  0.73 us (1%)
    pallas_call x1, Pallas kernels, body(): pl.pallas_call(functools.partial(step_kernel, n_gx, n_gy, margin), out_sh...  38 us
    pallas_call x1, Pallas kernels, body(): pl.pallas_call(functools.partial(halo_kernel, n_gx, n_gy, margin), out_sh...  18.7 us

profile of v6, /device:TPU:0, one launch (start us, length us, event | category | flops | bytes accessed | tf_op | source)
XLA Modules:
  0.0 59.4 jit_solution(4595252109191423809)
XLA Ops:
  0.6 0.0 copy-start.2
  0.6 0.0 copy-start
  0.7 0.0 copy-start.3
  0.7 0.0 copy-start.1
  0.7 18.7 %halo.1.ext = f32[2,4,512,128]{3,2,1,0:T(8,128)S(1)} custom-call(f32[2,256,256]{2,1,0:T(8,128)} %obj.1), custom_call_target="tpu_custom_call" | custom-call | tf_op jit(solution)/shard_map/halo/pallas_call | solution.py:560
  19.4 0.0 copy-done.2
  19.4 0.0 copy-done
  19.4 0.0 copy-done.3
  19.4 0.0 copy-done.1
  19.4 0.0 copy-start.4
  19.4 38.0 %step.1 = (f32[2,256,256]{2,1,0:T(8,128)S(1)}, f32[4,256,256]{2,1,0:T(8,128)S(1)}) custom-call(s32[1,2,4]{2,1,0:T(2,128)S(1)} %bitcast.5, f32[2,4,512,128]{3,2,1,0:T(8,128)S(1)} %halo.1.ext, f32[2,2,256,256]{3,2,1,0:T(8,128)S(1)} %copy-done, f32[4,256,256]{2,1,0:T(8,128)S(1)} %bitcast.3, bf16[256,512]{1,0:T(8,128)(2,1)S(1)} %copy-done.2), custom_call_target="tpu_custom_call" | custom-call | tf_op jit(solution)/shard_map/step/pallas_call | solution.py:573
  57.4 0.0 copy-done.4
  57.4 0.9 %add.6 = f32[2,256,256]{2,1,0:T(8,128)} add(f32[2,256,256]{2,1,0:T(8,128)S(1)} %copy-done.4, f32[2,256,256]{2,1,0:T(8,128)S(1)} %get-tuple-element.4) | non-fusion elementwise | flops 131072 | bytes 1572864 | tf_op jit(solution)/shard_map/add | solution.py:608
  58.3 1.1 %add.7 = f32[2,2,256,256]{3,2,1,0:T(8,128)} add(f32[2,2,256,256]{3,2,1,0:T(8,128)S(1)} %copy-done, f32[2,2,256,256]{3,2,1,0:T(8,128)S(1)} %bitcast.4) | non-fusion elementwise | flops 262144 | bytes 3145728 | tf_op jit(solution)/shard_map/add | solution.py:608
Async XLA Ops:
  0.6 18.8 %copy-start.2 = (bf16[256,512]{1,0:T(8,128)(2,1)S(1)}, bf16[256,512]{1,0:T(8,128)(2,1)}, u32[]{:S(2)}) copy-start(bf16[256,512]{1,0:T(8,128)(2,1)} %constant.2.clone.table) | copy-start | bytes 786436
  0.6 18.8 %copy-start = (f32[2,2,256,256]{3,2,1,0:T(8,128)S(1)}, f32[2,2,256,256]{3,2,1,0:T(8,128)}, u32[]{:S(2)}) copy-start(f32[2,2,256,256]{3,2,1,0:T(8,128)} %probe.1) | copy-start | bytes 3145732
  0.7 18.8 %copy-start.3 = (s32[4,1,2]{0,2,1:T(2,128)S(1)}, s32[4,1,2]{0,2,1:T(2,128)}, u32[]{:S(2)}) copy-start(s32[4,1,2]{0,2,1:T(2,128)} %param.8) | copy-start | bytes 100
  0.7 18.8 %copy-start.1 = (f32[4,1,256,256]{3,2,1,0:T(8,128)S(1)}, f32[4,1,256,256]{3,2,1,0:T(8,128)}, u32[]{:S(2)}) copy-start(f32[4,1,256,256]{3,2,1,0:T(8,128)} %param.7) | copy-start | bytes 3145732
  19.4 38.0 %copy-start.4 = (f32[2,256,256]{2,1,0:T(8,128)S(1)}, f32[2,256,256]{2,1,0:T(8,128)}, u32[]{:S(2)}) copy-start(f32[2,256,256]{2,1,0:T(8,128)} %obj.1) | copy-start | bytes 1572868

commit v7 on v6

--- a/solution.py
+++ b/solution.py
@@ -12,6 +12,7 @@
 MESH = pl.DeviceIdType.MESH
 VMEM = pl.BlockSpec(memory_space=pltpu.VMEM)
 HBM = pl.BlockSpec(memory_space=pltpu.MemorySpace.HBM)
+ANY = pl.BlockSpec(memory_space=pl.ANY)
 F32 = jnp.float32
 BF16 = jnp.bfloat16
 CHUNK = 32
@@ -22,6 +23,7 @@
 MIDS = 2
 LIMIT = 8 << 20
 STEP_LIMIT = 40 << 20
+EMIT_LIMIT = 2 << 20
 
 
 def dft_tables(extent):
@@ -238,7 +240,8 @@
         keep = rws(s["off"], s["n"])
         weight = s["src"][0, keep, :] + 1e-05
         for k in range(lo + first, hi):
-            out_probe[k - 1, keep, :] = s["src"][k, keep, :] / weight
+            mode, c = divmod(k - 1, 2)
+            out_probe[k - 1, keep, :] = probe[mode, c, keep, :] + s["src"][k, keep, :] / weight
 
     def planes_of(c):
         lo, hi = chunks[c][:2]
@@ -547,6 +550,16 @@
     assert not flight
     for copy in pending:
         copy.wait_send()
+
+
+def emit_kernel(obj, obj_step, probe, new_obj, new_probe, total, sems):
+    probe_out = pltpu.make_async_copy(probe, new_probe, sems.at[0])
+    probe_out.start()
+    total[...] = obj[...] + obj_step[...]
+    obj_out = pltpu.make_async_copy(total, new_obj, sems.at[1])
+    obj_out.start()
+    probe_out.wait()
+    obj_out.wait()
 
 
 def body(n_gx, n_gy, object_field, probe_field, amplitude, offsets):
@@ -605,7 +618,19 @@
         ),
         name="step",
     )(offsets.transpose(1, 2, 0), ext, probe_field, amplitude[:, 0], dft_tables(extent))
-    return object_field + out_obj, probe_field + out_probe.reshape(probe_field.shape)
+    new_obj, new_probe = pl.pallas_call(
+        emit_kernel,
+        out_shape=(
+            jax.ShapeDtypeStruct(object_field.shape, F32),
+            jax.ShapeDtypeStruct(out_probe.shape, F32),
+        ),
+        in_specs=[VMEM] * 3,
+        out_specs=(ANY, ANY),
+        scratch_shapes=[pltpu.VMEM(object_field.shape, F32), pltpu.SemaphoreType.DMA((2,))],
+        compiler_params=pltpu.CompilerParams(vmem_limit_bytes=EMIT_LIMIT),
+        name="emit",
+    )(object_field, out_obj, out_probe)
+    return new_obj, new_probe.reshape(probe_field.shape)
 
 
 def solution(mesh):

time: 59.5 us -> 58.6 us (0.985)
  other arithmetic: 1.97 us -> 0 us
  Pallas kernels: 56.7 us -> 57.6 us
    add x2 -> x0, other arithmetic: 1.97 us -> none  [the longest x1 1.1 us: body(): probe_field + out_probe.reshape(probe_field.shape)]
    pallas_call x0 -> x1, Pallas kernels: none -> 1.16 us  [body(): pl.pallas_call(emit_kernel, out_shape=(jax.ShapeDtypeStruct(object_field....]
where the time goes in v7:
time: 58.6 us; the launch traced here: 58.3 us
  Pallas kernels  57.6 us (98%)
  between operations  0.73 us (1%)
    pallas_call x1, Pallas kernels, body(): pl.pallas_call(functools.partial(step_kernel, n_gx, n_gy, margin), out_sh...  37.7 us
    pallas_call x1, Pallas kernels, body(): pl.pallas_call(functools.partial(halo_kernel, n_gx, n_gy, margin), out_sh...  18.7 us

profile of v7, /device:TPU:0, one launch (start us, length us, event | category | flops | bytes accessed | tf_op | source)
XLA Modules:
  0.0 58.3 jit_solution(10782363275465178986)
XLA Ops:
  0.6 0.0 copy-start.3
  0.6 0.0 copy-start.4
  0.7 0.0 copy-start.2
  0.7 0.0 copy-start.1
  0.7 18.7 %halo.1.ext = f32[2,4,512,128]{3,2,1,0:T(8,128)S(1)} custom-call(f32[2,256,256]{2,1,0:T(8,128)} %obj.3), custom_call_target="tpu_custom_call" | custom-call | tf_op jit(solution)/shard_map/halo/pallas_call | solution.py:573
  19.4 0.0 copy-done.3
  19.4 0.0 copy-done.4
  19.4 0.0 copy-done.2
  19.4 0.0 copy-done.1
  19.4 0.0 copy-start
  19.4 37.7 %step.1 = (f32[2,256,256]{2,1,0:T(8,128)S(1)}, f32[4,256,256]{2,1,0:T(8,128)S(1)}) custom-call(s32[1,2,4]{2,1,0:T(2,128)S(1)} %bitcast.4, f32[2,4,512,128]{3,2,1,0:T(8,128)S(1)} %halo.1.ext, f32[2,2,256,256]{3,2,1,0:T(8,128)S(1)} %copy-done.1, f32[4,256,256]{2,1,0:T(8,128)S(1)} %bitcast.3, bf16[256,512]{1,0:T(8,128)(2,1)S(1)} %copy-done.3), custom_call_target="tpu_custom_call" | custom-call | tf_op jit(solution)/shard_map/step/pallas_call | solution.py:586
  57.1 0.0 copy-done
  57.1 1.2 %emit.1 = (f32[2,256,256]{2,1,0:T(8,128)}, f32[4,256,256]{2,1,0:T(8,128)}) custom-call(f32[2,256,256]{2,1,0:T(8,128)S(1)} %copy-done, f32[2,256,256]{2,1,0:T(8,128)S(1)} %get-tuple-element.6.obj_step, f32[4,256,256]{2,1,0:T(8,128)S(1)} %get-tuple-element.7.probe), custom_call_target="tpu_custom_call" | custom-call | tf_op jit(solution)/shard_map/emit/pallas_call | solution.py:621
Async XLA Ops:
  0.6 18.8 %copy-start.3 = (bf16[256,512]{1,0:T(8,128)(2,1)S(1)}, bf16[256,512]{1,0:T(8,128)(2,1)}, u32[]{:S(2)}) copy-start(bf16[256,512]{1,0:T(8,128)(2,1)} %constant.2.clone.table) | copy-start | bytes 786436
  0.6 18.8 %copy-start.4 = (s32[4,1,2]{0,2,1:T(2,128)S(1)}, s32[4,1,2]{0,2,1:T(2,128)}, u32[]{:S(2)}) copy-start(s32[4,1,2]{0,2,1:T(2,128)} %param.8) | copy-start | bytes 100
  0.7 18.8 %copy-start.2 = (f32[4,1,256,256]{3,2,1,0:T(8,128)S(1)}, f32[4,1,256,256]{3,2,1,0:T(8,128)}, u32[]{:S(2)}) copy-start(f32[4,1,256,256]{3,2,1,0:T(8,128)} %param.7) | copy-start | bytes 3145732
  0.7 18.8 %copy-start.1 = (f32[2,2,256,256]{3,2,1,0:T(8,128)S(1)}, f32[2,2,256,256]{3,2,1,0:T(8,128)}, u32[]{:S(2)}) copy-start(f32[2,2,256,256]{3,2,1,0:T(8,128)} %probe.1) | copy-start | bytes 3145732
  19.4 37.7 %copy-start = (f32[2,256,256]{2,1,0:T(8,128)S(1)}, f32[2,256,256]{2,1,0:T(8,128)}, u32[]{:S(2)}) copy-start(f32[2,256,256]{2,1,0:T(8,128)} %obj.3) | copy-start | bytes 1572868
